TPU v7x, 32 devices: a whole 2x2x4 slice. The times are simulated.
32 devices in a mesh: mesh: 16 (over z, y, core), band: 2 (over x).
Axes of the slice: x: 2, y: 2, z: 4, core: 2. Of those that a mesh axis runs over, the one named last changes fastest.
Arguments:
- psi: bfloat16 [16, 286720], P('band', 'mesh'), may hold values from -9 to 9
- cell_nodes: int32 [216, 128], replicated, may hold values from 0 to 19711, as said below
- cell_scale: float32 [2048], P('mesh'), may hold values from 0.5 to 2
- cell_matrix: bfloat16 [216, 216], replicated, may hold values from -1 to 2
- node_potential: bfloat16 [286720], P('mesh'), may hold values from -1.5 to 0.5
- proj_values: bfloat16 [216, 8, 2048], P(None, None, 'mesh'), may hold values from -1 to 1
- entry_cell: int32 [2048], P('mesh'), may hold values from 0 to 127
- entry_atom: int32 [2048], P('mesh'), may hold values from -1 to 191, as said below
- coupling: float32 [1024, 8, 8], P('mesh'), may hold values from -3 to 3
Outputs:
- filtered: bfloat16 [16, 286720], P('band', 'mesh')
- correlation: float32 [16, 16], replicated
Inputs may be any that keep to these rules, and one draw needn't show every extreme that they name: `cell_nodes`: node j = 36 a + 6 b + c of a cell is its local node (a, b, c) in the order the cell_matrix uses; cells that share a node give it the same number; values 17920 + i name node i of the next partition, and only nodes below 1792 of a partition are named so by the previous one. `entry_atom`: live entries of a partition come first, then -1 padding; the number of live entries differs between partitions.
All inputs are finite; a program needn't handle non-finite values.
Results may differ from a plain program's by a relative error of at most 0.0022.
Values may be sent and summed in bfloat16 or wider, within the bound.
A program may use at most 128 MiB of HBM per device.

v0:
```python
import jax
import jax.numpy as jnp
from jax import lax
from jax.sharding import PartitionSpec as P

FACEP = 1792


CENTER = 0.5
HALFWIDTH = 2.5
HIGH = lax.Precision.HIGHEST


def from_behind(value, axis, steps):
    count = lax.axis_size(axis)
    pairs = [(source, (source + steps) % count) for source in range(count)]
    return lax.ppermute(value, axis, pairs)


def padded(block, sides, width):
    for axis, dim in sides:
        count = lax.axis_size(axis)
        forward = [(i, i + 1) for i in range(count - 1)]
        forward.append((count - 1, 0))
        backward = [(target, source) for source, target in forward]
        low = lax.ppermute(
            lax.slice_in_dim(block, block.shape[dim] - width, None, axis=dim), axis, forward
        )
        high = lax.ppermute(lax.slice_in_dim(block, 0, width, axis=dim), axis, backward)
        block = jnp.concatenate([low, block, high], axis=dim)
    return block


def local(
    psi,
    cell_nodes,
    cell_scale,
    cell_matrix,
    node_potential,
    proj_values,
    entry_cell,
    entry_atom,
    coupling,
):
    states = psi.shape[0]
    node_count = psi.shape[1]
    atom_count = coupling.shape[0]
    proj_count = coupling.shape[1]
    entry_count = entry_atom.shape[0]
    entry_nodes = cell_nodes[:, entry_cell]
    slot_ids = jnp.arange(3 * atom_count, dtype=jnp.int32)
    selector = (entry_atom[:, None] == slot_ids[None, :]).astype(jnp.float32)
    proj_wide = proj_values.astype(jnp.float32)
    potential = node_potential.astype(jnp.float32) - CENTER

    def apply_filter(field):
        ghost = from_behind(field[:, :FACEP], "mesh", -1)
        extended = jnp.concatenate([field, ghost], axis=1)
        entry_vals = extended[:, entry_nodes]
        partial_sum = jnp.einsum(
            "jke,sje->esk", proj_values, entry_vals, preferred_element_type=jnp.float32
        )
        partial_sum = partial_sum.reshape(entry_count, states * proj_count)
        grouped = jnp.dot(selector.T, partial_sum, precision=HIGH).reshape(
            3, atom_count, states * proj_count
        )
        rim_rows = padded(grouped, (("mesh", 0),), 1)
        coefficient = (rim_rows[0] + rim_rows[2] + rim_rows[4]).reshape(
            atom_count, states, proj_count
        )
        atom_vals = jnp.einsum("akl,asl->ask", coupling, coefficient, precision=HIGH)
        atom_vals = atom_vals.reshape(1, atom_count, states * proj_count)
        beside_all = padded(atom_vals, (("mesh", 0),), 1)
        beside_all = beside_all.reshape(3 * atom_count, states * proj_count)
        entry_terms = jnp.dot(selector, beside_all, precision=HIGH).reshape(
            entry_count, states, proj_count
        )
        node_terms = jnp.einsum("jke,esk->sje", proj_wide, entry_terms, precision=HIGH)
        cell_vals = extended[:, cell_nodes]
        cell_terms = (
            jnp.einsum("ij,sjc->sic", cell_matrix, cell_vals, preferred_element_type=jnp.float32)
            * cell_scale
        )
        summed = jnp.zeros((states, node_count + FACEP), jnp.float32)
        summed = summed.at[:, cell_nodes].add(cell_terms)
        summed = summed.at[:, entry_nodes].add(node_terms)
        returned = from_behind(summed[:, node_count:], "mesh", 1)
        assembled = summed[:, :node_count].at[:, :FACEP].add(returned)
        return (assembled + potential * field.astype(jnp.float32)) / HALFWIDTH

    first_step = apply_filter(psi).astype(jnp.bfloat16)
    filtered = (2.0 * apply_filter(first_step) - psi.astype(jnp.float32)).astype(jnp.bfloat16)
    scale_all = 1.0 / (lax.axis_size("mesh") * node_count)
    all_states = lax.all_gather(filtered, "band", axis=0, tiled=True)
    local_sum = lax.dot_general(
        all_states, all_states, (((1,), (1,)), ((), ())), preferred_element_type=jnp.float32
    )
    correlation = lax.psum(local_sum, "mesh") * scale_all
    return (filtered, correlation)


def solution(mesh):
    return jax.shard_map(
        local,
        mesh=mesh,
        in_specs=(
            P("band", "mesh"),
            P(),
            P("mesh"),
            P(),
            P("mesh"),
            P(None, None, "mesh"),
            P("mesh"),
            P("mesh"),
            P("mesh", None, None),
        ),
        out_specs=(P("band", "mesh"), P()),
        check_vma=False,
    )
```

profile of v0, /device:TPU:0, one launch (start us, length us, event | category | flops | bytes accessed | tf_op | source)
XLA Modules:
  0.0 1147.2 jit_solution(18365605003493958822)
XLA Ops:
  1.4 5.5 collective-permute-start
  16.9 95.6 %gather_fusion.2 = bf16[27648,8]{1,0:T(8,128)(2,1)} fusion(bf16[8,19712]{0,1:T(8,128)(2,1)} %copy.214, s32[27648]{0:T(1024)S(1)} %broadcast_clamp_fusion), kind=kCustom, calls=%fused_computation.2 | custom fusion | bytes 995328 | tf_op jit(solution)/shard_map/gather | solution.py:59
  112.5 6.7 copy.220
  121.0 95.6 %gather_fusion = bf16[27648,8]{1,0:T(8,128)(2,1)} fusion(bf16[8,19712]{0,1:T(8,128)(2,1)} %copy.214, s32[27648]{0:T(1024)S(1)} %broadcast_clamp_fusion.1), kind=kCustom, calls=%fused_computation | custom fusion | bytes 995328 | tf_op jit(solution)/shard_map/gather | solution.py:79
  216.6 5.7 copy.215
  228.0 7.2 copy.254
  235.2 151.6 %scatter_custom_fusion = f32[8,19712]{0,1:T(8,128)} fusion(s32[27648]{0:T(1024)S(1)} %fusion.16, f32[27648,8]{1,0:T(8,128)} %bitcast.108, f32[]{:T(128)} %constant.60.clone.1), kind=kCustom, calls=%fused_computation.11 | custom fusion | flops 221184 | bytes 631296 | tf_op jit(solution)/shard_map/scatter-add | solution.py:85
  388.6 8.0 copy.231
  396.6 139.9 %scatter_fusion = f32[8,19712]{0,1:T(8,128)} fusion(f32[8,19712]{0,1:T(8,128)} %scatter_custom_fusion, s32[27648]{0:T(1024)S(1)} %bitcast.115, f32[27648,8]{1,0:T(8,128)} %copy.231), kind=kCustom, calls=%fused_computation.6 | custom fusion | flops 221184 | bytes 2764800 | tf_op jit(solution)/shard_map/scatter-add | solution.py:86
  539.0 8.2 slice.121
  547.3 5.4 copy.256
  553.8 4.5 collective-permute-start.6
  563.7 95.6 %gather_fusion.4 = bf16[27648,8]{1,0:T(8,128)(2,1)} fusion(bf16[8,19712]{0,1:T(8,128)(2,1)} %copy.235, s32[27648]{0:T(1024)S(1)} %copy-done.4), kind=kCustom, calls=%fused_computation.4 | custom fusion | bytes 995328 | tf_op jit(solution)/shard_map/gather | solution.py:59
  659.3 6.7 copy.239
  671.2 95.6 %gather_fusion.3 = bf16[27648,8]{1,0:T(8,128)(2,1)} fusion(bf16[8,19712]{0,1:T(8,128)(2,1)} %copy.235, s32[27648]{0:T(1024)S(1)} %copy-done.6), kind=kCustom, calls=%fused_computation.3 | custom fusion | bytes 995328 | tf_op jit(solution)/shard_map/gather | solution.py:79
  766.8 5.7 copy.236
  778.2 7.2 copy.255
  785.4 151.5 %scatter_custom_fusion.2 = f32[8,19712]{0,1:T(8,128)} fusion(s32[27648]{0:T(1024)} %copy-done.10, f32[27648,8]{1,0:T(8,128)} %bitcast.107, f32[]{:T(128)} %constant.60.clone.1), kind=kCustom, calls=%fused_computation.9 | custom fusion | flops 221184 | bytes 631296 | tf_op jit(solution)/shard_map/scatter-add | solution.py:85
  938.7 8.0 copy.250
  946.7 139.9 %scatter_fusion.1 = f32[8,19712]{0,1:T(8,128)} fusion(f32[8,19712]{0,1:T(8,128)} %scatter_custom_fusion.2, s32[27648]{0:T(1024)S(1)} %bitcast.116, f32[27648,8]{1,0:T(8,128)} %copy.250), kind=kCustom, calls=%fused_computation.8 | custom fusion | flops 221184 | bytes 2764800 | tf_op jit(solution)/shard_map/scatter-add | solution.py:86
  1088.5 8.2 slice.128
  1096.7 5.4 copy.258
  1103.2 7.3 all_gather.3
  1110.9 35.7 %psum.7 = f32[16,16]{1,0:T(8,128)S(1)} all-reduce(f32[16,16]{1,0:T(8,128)S(1)} %fusion.44), channel_id=1, replica_groups=mesh['mesh'=16,'band'=2] {'mesh'}, use_global_device_ids=true, to_apply=%region_5.0 | all-reduce | flops 256 | bytes 2048 | tf_op jit(solution)/shard_map/psum | solution.py:98
  (115 shorter events, 45.5 us)
Async XLA Ops:
  0.6 227.1 %copy-start = (bf16[216,216]{1,0:T(8,128)(2,1)S(1)}, bf16[216,216]{1,0:T(8,128)(2,1)}, u32[]{:S(2)}) copy-start(bf16[216,216]{1,0:T(8,128)(2,1)} %param.16) | copy-start | bytes 279940
  1.4 10.6 collective-permute-start
  7.8 227.4 %copy-start.10 = (s32[27648]{0:T(1024)}, s32[27648]{0:T(1024)S(1)}, u32[]{:S(2)}) copy-start(s32[27648]{0:T(1024)S(1)} %fusion.16) | copy-start | bytes 331780
  10.4 102.1 %copy-start.3 = (s32[27648]{0:T(1024)}, s32[27648]{0:T(1024)S(1)}, u32[]{:S(2)}) copy-start(s32[27648]{0:T(1024)S(1)} %broadcast_clamp_fusion) | copy-start | bytes 331780
  12.0 107.6 %copy-start.14 = (s32[128]{0:T(128)S(1)}, s32[128]{0:T(128)}, u32[]{:S(2)}) copy-start(s32[128]{0:T(128)} %param.20) | copy-start | bytes 1540
  12.1 108.7 %copy-start.7 = (s32[216,128]{1,0:T(8,128)S(1)}, s32[216,128]{1,0:T(8,128)}, u32[]{:S(2)}) copy-start(s32[216,128]{1,0:T(8,128)} %param.14) | copy-start | bytes 331780
  12.1 108.8 %copy-start.12 = (f32[64,8,8]{0,2,1:T(8,128)S(1)}, f32[64,8,8]{0,2,1:T(8,128)}, u32[]{:S(2)}) copy-start(f32[64,8,8]{0,2,1:T(8,128)} %param.21) | copy-start | bytes 49156
  112.5 115.2 %copy-start.13 = (f32[128]{0:T(128)S(1)}, f32[128]{0:T(128)}, u32[]{:S(2)}) copy-start(f32[128]{0:T(128)} %param.15) | copy-start | bytes 1540
  120.0 102.3 %collective-permute-start.2 = (f32[1,64,64]{1,2,0:T(8,128)S(1)}, f32[1,64,64]{1,2,0:T(8,128)S(1)}, u32[]{:S(2)}, u32[]{:S(2)}) collective-permute-start(f32[1,64,64]{1,2,0:T(8,128)S(1)} %get-tuple-element.43), channel_id=1, source_target_pairs={{2,0},{4,2},{6,4},{8,6},{10,8},{12,10},{14,12},{16,14},{18,16},{20... | collective-permute-start | bytes 49160 | tf_op jit(solution)/shard_map/ppermute | solution.py:29
  120.8 101.5 %collective-permute-start.1 = (f32[1,64,64]{1,2,0:T(8,128)S(1)}, f32[1,64,64]{1,2,0:T(8,128)S(1)}, u32[]{:S(2)}, u32[]{:S(2)}) collective-permute-start(f32[1,64,64]{1,2,0:T(8,128)S(1)} %get-tuple-element.42), channel_id=1, source_target_pairs={{0,2},{2,4},{4,6},{6,8},{8,10},{10,12},{12,14},{14,16},{16,18},{18... | collective-permute-start | bytes 49160 | tf_op jit(solution)/shard_map/ppermute | solution.py:26
  120.8 101.5 %copy-start.5 = (s32[27648]{0:T(1024)}, s32[27648]{0:T(1024)S(1)}, u32[]{:S(2)}) copy-start(s32[27648]{0:T(1024)S(1)} %broadcast_clamp_fusion.1) | copy-start | bytes 331780
  223.2 163.6 %collective-permute-start.4 = (f32[1,64,64]{1,2,0:T(8,128)S(1)}, f32[1,64,64]{1,2,0:T(8,128)S(1)}, u32[]{:S(2)}, u32[]{:S(2)}) collective-permute-start(f32[1,64,64]{1,2,0:T(8,128)S(1)} %bitcast.122), channel_id=1, source_target_pairs={{2,0},{4,2},{6,4},{8,6},{10,8},{12,10},{14,12},{16,14},{18,16},{20... | collective-permute-start | bytes 49160 | tf_op jit(solution)/shard_map/ppermute | solution.py:29
  227.7 159.1 %collective-permute-start.3 = (f32[1,64,64]{1,2,0:T(8,128)S(1)}, f32[1,64,64]{1,2,0:T(8,128)S(1)}, u32[]{:S(2)}, u32[]{:S(2)}) collective-permute-start(f32[1,64,64]{1,2,0:T(8,128)S(1)} %bitcast.123), channel_id=1, source_target_pairs={{0,2},{2,4},{4,6},{6,8},{8,10},{10,12},{12,14},{14,16},{16,18},{18... | collective-permute-start | bytes 49160 | tf_op jit(solution)/shard_map/ppermute | solution.py:26
  396.6 141.8 %copy-start.11 = (bf16[17920]{0:T(1024)(128)(2,1)S(1)}, bf16[17920]{0:T(1024)(128)(2,1)}, u32[]{:S(2)}) copy-start(bf16[17920]{0:T(1024)(128)(2,1)} %param.17) | copy-start | bytes 107524
  538.3 14.7 %collective-permute-start.5 = (f32[8,1792]{1,0:T(8,128)S(1)}, f32[8,1792]{1,0:T(8,128)S(1)}, u32[]{:S(2)}, u32[]{:S(2)}) collective-permute-start(f32[8,1792]{1,0:T(8,128)S(1)} %copy.234), channel_id=1, source_target_pairs={{0,2},{2,4},{4,6},{6,8},{8,10},{10,12},{12,14},{14,16},{16,18},{18... | collective-permute-start | bytes 172040 | tf_op jit(solution)/shard_map/ppermute | solution.py:17
  547.3 16.5 %copy-start.4 = (s32[27648]{0:T(1024)S(1)}, s32[27648]{0:T(1024)}, u32[]{:S(2)}) copy-start(s32[27648]{0:T(1024)} %copy-done.3) | copy-start | bytes 331780
  553.8 117.4 %copy-start.6 = (s32[27648]{0:T(1024)S(1)}, s32[27648]{0:T(1024)}, u32[]{:S(2)}) copy-start(s32[27648]{0:T(1024)} %copy-done.5) | copy-start | bytes 331780
  553.8 6.1 collective-permute-start.6
  666.7 105.8 %collective-permute-start.8 = (f32[1,64,64]{1,2,0:T(8,128)S(1)}, f32[1,64,64]{1,2,0:T(8,128)S(1)}, u32[]{:S(2)}, u32[]{:S(2)}) collective-permute-start(f32[1,64,64]{1,2,0:T(8,128)S(1)} %get-tuple-element.41), channel_id=1, source_target_pairs={{2,0},{4,2},{6,4},{8,6},{10,8},{12,10},{14,12},{16,14},{18,16},{20... | collective-permute-start | bytes 49160 | tf_op jit(solution)/shard_map/ppermute | solution.py:29
  671.2 101.3 %collective-permute-start.7 = (f32[1,64,64]{1,2,0:T(8,128)S(1)}, f32[1,64,64]{1,2,0:T(8,128)S(1)}, u32[]{:S(2)}, u32[]{:S(2)}) collective-permute-start(f32[1,64,64]{1,2,0:T(8,128)S(1)} %get-tuple-element.40), channel_id=1, source_target_pairs={{0,2},{2,4},{4,6},{6,8},{8,10},{10,12},{12,14},{14,16},{16,18},{18... | collective-permute-start | bytes 49160 | tf_op jit(solution)/shard_map/ppermute | solution.py:26
  773.4 163.5 %collective-permute-start.10 = (f32[1,64,64]{1,2,0:T(8,128)S(1)}, f32[1,64,64]{1,2,0:T(8,128)S(1)}, u32[]{:S(2)}, u32[]{:S(2)}) collective-permute-start(f32[1,64,64]{1,2,0:T(8,128)S(1)} %bitcast.119), channel_id=1, source_target_pairs={{2,0},{4,2},{6,4},{8,6},{10,8},{12,10},{14,12},{16,14},{18,16},{20... | collective-permute-start | bytes 49160 | tf_op jit(solution)/shard_map/ppermute | solution.py:29
  777.9 159.0 %collective-permute-start.9 = (f32[1,64,64]{1,2,0:T(8,128)S(1)}, f32[1,64,64]{1,2,0:T(8,128)S(1)}, u32[]{:S(2)}, u32[]{:S(2)}) collective-permute-start(f32[1,64,64]{1,2,0:T(8,128)S(1)} %bitcast.120), channel_id=1, source_target_pairs={{0,2},{2,4},{4,6},{6,8},{8,10},{10,12},{12,14},{14,16},{16,18},{18... | collective-permute-start | bytes 49160 | tf_op jit(solution)/shard_map/ppermute | solution.py:26
  1088.5 13.9 %collective-permute-start.11 = (f32[8,1792]{1,0:T(8,128)S(1)}, f32[8,1792]{1,0:T(8,128)S(1)}, u32[]{:S(2)}, u32[]{:S(2)}) collective-permute-start(f32[8,1792]{1,0:T(8,128)S(1)} %copy.253), channel_id=1, source_target_pairs={{0,2},{2,4},{4,6},{6,8},{8,10},{10,12},{12,14},{14,16},{16,18},{18... | collective-permute-start | bytes 172040 | tf_op jit(solution)/shard_map/ppermute | solution.py:17
  1103.2 43.9 %copy-start.2 = (bf16[8,17920]{1,0:T(8,128)(2,1)}, bf16[8,17920]{1,0:T(8,128)(2,1)S(1)}, u32[]{:S(2)}) copy-start(bf16[8,17920]{1,0:T(8,128)(2,1)S(1)} %fusion.9) | copy-start | bytes 860164
  (3 other events, 44.6 us)
where the time goes:
time: 1150 us
  other arithmetic  589 us (51%)
  local copies, waits for them, and re-layouts  484 us (42%)
  blocking collectives  43 us (4%)
  starting transfers between devices  24.3 us (2%)
    scatter-add x2, other arithmetic, apply_filter(): summed = summed.at[:, cell_nodes].add(cell_terms)  303 us
    scatter-add x2, other arithmetic, apply_filter(): summed = summed.at[:, entry_nodes].add(node_terms)  280 us
    gather x4, local copies, waits for them, and re-layouts, apply_filter(): entry_vals = extended[:, entry_nodes]  204 us
    gather x4, local copies, waits for them, and re-layouts, apply_filter(): cell_vals = extended[:, cell_nodes]  203 us
    psum x1, blocking collectives, local(): correlation = lax.psum(local_sum, 'mesh') * scale_all  35.7 us
  transfers between devices with their start and end apart: 12, of which 1 were waited for; matrix products, arithmetic and copies ran while one was open for 48% of the time, Pallas kernels for 0%

commit v1 on v0

v1 whole, which is shorter than its diff:
```python
import functools

import jax
import jax.numpy as jnp
from jax import lax
from jax.experimental import pallas as pl
from jax.experimental.pallas import tpu as pltpu
from jax.sharding import PartitionSpec as P

FACEP = 1792
CENTER = 0.5
HALFWIDTH = 2.5
HIGH = lax.Precision.HIGHEST
WIDE = 256
GROUP = 12
F32 = jnp.float32
BF16 = jnp.bfloat16


def from_behind(value, axis, steps):
    count = lax.axis_size(axis)
    pairs = [(source, (source + steps) % count) for source in range(count)]
    return lax.ppermute(value, axis, pairs)


def fill_onehot(cn_ref, group, oh_ref):
    rows = cn_ref[group]
    hi = jnp.bitwise_and(rows, WIDE - 1)
    lanes = rows.shape[1]
    iota = lax.broadcasted_iota(jnp.int32, (WIDE, lanes), 0)
    for jj in range(GROUP):
        oh_ref[:, jj * lanes:(jj + 1) * lanes] = jnp.where(
            iota == hi[jj:jj + 1, :], 1.0, 0.0
        ).astype(BF16)
    return lax.shift_right_logical(rows, 8)


def gather_kernel(flags_ref, cn_ref, ext_ref, kmat_ref, scale_ref, proj_ref, ecell_ref,
                  eatom_ref, ct_ref, grouped_ref, lhs_ref, oh_ref, xs_ref, es_ref):
    states = ext_ref.shape[0]
    chunks, rows_in_chunk, _ = lhs_ref.shape
    layers = rows_in_chunk // states
    groups = cn_ref.shape[0]
    cells = cn_ref.shape[2]
    width = groups * GROUP
    for c in range(chunks):
        base = c * layers * WIDE
        parts = [
            ext_ref[:, base + l * WIDE:base + (l + 1) * WIDE].astype(F32) for l in range(layers)
        ]
        lhs_ref[c] = jnp.concatenate(parts, axis=0).astype(BF16)

    def group_body(g, carry):
        lo = fill_onehot(cn_ref, g, oh_ref)

        def chunk_body(c, inner):
            @pl.when(flags_ref[g * chunks + c] > 0)
            def _():
                out = jnp.dot(lhs_ref[c], oh_ref[...], preferred_element_type=F32)
                for jj in range(GROUP):
                    where = pl.ds(pl.multiple_of((g * GROUP + jj) * states, states), states)
                    value = xs_ref[where, :]
                    row = lo[jj:jj + 1, :] - c * layers
                    for l in range(layers):
                        value = jnp.where(
                            row == l,
                            out[l * states:(l + 1) * states, jj * cells:(jj + 1) * cells],
                            value,
                        )
                    xs_ref[where, :] = value
            return inner

        return lax.fori_loop(0, chunks, chunk_body, carry)

    xs_ref[...] = jnp.zeros_like(xs_ref)
    lax.fori_loop(0, groups, group_body, 0)

    cell_ids = lax.broadcasted_iota(jnp.int32, (cells, ecell_ref.shape[1]), 0)
    spread = jnp.where(cell_ids == ecell_ref[...], 1.0, 0.0).astype(BF16)
    es_ref[...] = jnp.dot(xs_ref[...].astype(BF16), spread, preferred_element_type=F32)

    kmat = kmat_ref[...]
    scale = scale_ref[...]
    for s in range(0, states, 2):
        pair = jnp.concatenate(
            [xs_ref[pl.ds(s, width, stride=states), :], xs_ref[pl.ds(s + 1, width, stride=states), :]],
            axis=1,
        ).astype(BF16)
        out = jnp.dot(kmat, pair, preferred_element_type=F32)
        ct_ref[pl.ds(s, width, stride=states), :] = out[:, :cells] * scale
        ct_ref[pl.ds(s + 1, width, stride=states), :] = out[:, cells:] * scale

    nproj = proj_ref.shape[1]
    entries = ecell_ref.shape[1]

    def partial_body(j, accs):
        values = es_ref[pl.ds(pl.multiple_of(j * states, states), states), :]
        proj = proj_ref[j].astype(F32)
        return tuple(acc + proj[k:k + 1, :] * values for k, acc in enumerate(accs))

    zero = jnp.zeros((states, entries), F32)
    accs = lax.fori_loop(0, width, partial_body, (zero,) * nproj, unroll=4)
    partial_sum = jnp.concatenate(accs, axis=0)
    atoms = grouped_ref.shape[2]
    slot_ids = lax.broadcasted_iota(jnp.int32, (atoms, entries), 0)
    for g in range(3):
        chosen = jnp.where(eatom_ref[...] == slot_ids + g * atoms, 1.0, 0.0)
        grouped_ref[g] = lax.dot_general(
            partial_sum, chosen, (((1,), (1,)), ((), ())), precision=HIGH,
            preferred_element_type=F32,
        )


def scatter_kernel(flags_ref, cn_ref, ct_ref, coef_ref, coup_ref, proj_ref, ecell_ref,
                   eatom_ref, y_ref, oh_ref, ns_ref, v_ref, lhs_ref, acc_ref):
    chunks, rows_in_chunk, _ = acc_ref.shape
    groups = cn_ref.shape[0]
    cells = cn_ref.shape[2]
    width = groups * GROUP
    states = ct_ref.shape[0] // width
    layers = rows_in_chunk // (2 * states)
    nproj = proj_ref.shape[1]
    entries = ecell_ref.shape[1]
    atoms = coef_ref.shape[2]
    slot_ids = lax.broadcasted_iota(jnp.int32, (atoms, entries), 0)
    entry_terms = jnp.zeros((nproj * states, entries), F32)
    for g in range(3):
        rows = []
        for k in range(nproj):
            acc = jnp.zeros((states, atoms), F32)
            for l in range(nproj):
                acc = acc + (
                    coup_ref[g, k * nproj + l:k * nproj + l + 1, :]
                    * coef_ref[g, l * states:(l + 1) * states, :]
                )
            rows.append(acc)
        chosen = jnp.where(eatom_ref[...] == slot_ids + g * atoms, 1.0, 0.0)
        entry_terms = entry_terms + jnp.dot(
            jnp.concatenate(rows, axis=0), chosen, precision=HIGH, preferred_element_type=F32
        )
    terms = [entry_terms[k * states:(k + 1) * states, :] for k in range(nproj)]

    def node_body(j, carry):
        proj = proj_ref[j].astype(F32)
        total = proj[0:1, :] * terms[0]
        for k in range(1, nproj):
            total = total + proj[k:k + 1, :] * terms[k]
        ns_ref[pl.ds(pl.multiple_of(j * states, states), states), :] = total
        return carry

    lax.fori_loop(0, width, node_body, 0, unroll=4)
    cell_ids = lax.broadcasted_iota(jnp.int32, (cells, entries), 0)
    spread = jnp.where(cell_ids == ecell_ref[...], 1.0, 0.0).astype(BF16)
    back = (((1,), (1,)), ((), ()))
    node_vals = ns_ref[...]
    node_top = node_vals.astype(BF16)
    node_rest = (node_vals - node_top.astype(F32)).astype(BF16)
    v_ref[...] = (
        ct_ref[...]
        + lax.dot_general(node_top, spread, back, preferred_element_type=F32)
        + lax.dot_general(node_rest, spread, back, preferred_element_type=F32)
    )
    acc_ref[...] = jnp.zeros_like(acc_ref)

    def group_body(g, carry):
        lo = fill_onehot(cn_ref, g, oh_ref)

        def chunk_body(c, inner):
            @pl.when(flags_ref[g * chunks + c] > 0)
            def _():
                for jj in range(GROUP):
                    start = pl.multiple_of((g * GROUP + jj) * states, states)
                    value = v_ref[pl.ds(start, states), :]
                    top = value.astype(BF16).astype(F32)
                    both = jnp.concatenate([top, value - top], axis=0)
                    row = lo[jj:jj + 1, :] - c * layers
                    for l in range(layers):
                        lhs_ref[l * 2 * states:(l + 1) * 2 * states, jj * cells:(jj + 1) * cells] = (
                            jnp.where(row == l, both, 0.0).astype(BF16)
                        )
                acc_ref[c] += lax.dot_general(
                    lhs_ref[...], oh_ref[...], back, preferred_element_type=F32
                )
            return inner

        return lax.fori_loop(0, chunks, chunk_body, carry)

    lax.fori_loop(0, groups, group_body, 0)
    for c in range(chunks):
        for l in range(layers):
            base = (c * layers + l) * WIDE
            at = l * 2 * states
            y_ref[:, base:base + WIDE] = (
                acc_ref[c, at:at + states, :] + acc_ref[c, at + states:at + 2 * states, :]
            )


def local(
    psi,
    cell_nodes,
    cell_scale,
    cell_matrix,
    node_potential,
    proj_values,
    entry_cell,
    entry_atom,
    coupling,
):
    states, node_count = psi.shape
    width, cells = cell_nodes.shape
    atoms, nproj, _ = coupling.shape
    entries = entry_atom.shape[0]
    full = node_count + FACEP
    chunks = full // FACEP
    layers = FACEP // WIDE
    groups = width // GROUP
    span = GROUP * cells

    table = cell_nodes.reshape(groups, GROUP, cells)
    owner = table // FACEP
    flags = jnp.stack(
        [jnp.any(owner == c, axis=(1, 2)) for c in range(chunks)], axis=1
    ).astype(jnp.int32).reshape(groups * chunks)
    scale_row = cell_scale.reshape(1, cells)
    ecell = entry_cell.reshape(1, entries)
    eatom = entry_atom.reshape(1, entries)
    coup = coupling.transpose(1, 2, 0).reshape(nproj * nproj, atoms)
    coup_all = jnp.stack([from_behind(coup, "mesh", 1), coup, from_behind(coup, "mesh", -1)])
    pot_ghost = from_behind(node_potential[:FACEP], "mesh", -1)
    potential = jnp.concatenate([node_potential, pot_ghost]).astype(F32) - CENTER

    vmem = pl.BlockSpec(memory_space=pltpu.VMEM)
    smem = pl.BlockSpec(memory_space=pltpu.SMEM)

    gather = pl.pallas_call(
        gather_kernel,
        out_shape=(
            jax.ShapeDtypeStruct((width * states, cells), F32),
            jax.ShapeDtypeStruct((3, nproj * states, atoms), F32),
        ),
        in_specs=[smem] + [vmem] * 7,
        out_specs=(vmem, vmem),
        scratch_shapes=[
            pltpu.VMEM((chunks, layers * states, WIDE), BF16),
            pltpu.VMEM((WIDE, span), BF16),
            pltpu.VMEM((width * states, cells), F32),
            pltpu.VMEM((width * states, entries), F32),
        ],
        name="gather_cells",
    )
    scatter = pl.pallas_call(
        scatter_kernel,
        out_shape=jax.ShapeDtypeStruct((states, full), F32),
        in_specs=[smem] + [vmem] * 7,
        out_specs=vmem,
        scratch_shapes=[
            pltpu.VMEM((WIDE, span), BF16),
            pltpu.VMEM((width * states, entries), F32),
            pltpu.VMEM((width * states, cells), F32),
            pltpu.VMEM((layers * 2 * states, span), BF16),
            pltpu.VMEM((chunks, layers * 2 * states, WIDE), F32),
        ],
        name="scatter_nodes",
    )

    def assemble(extended):
        cell_terms, grouped = gather(
            flags, table, extended, cell_matrix, scale_row, proj_values, ecell, eatom
        )
        ahead1 = from_behind(grouped[1:], "mesh", 1)
        back1 = from_behind(grouped[:2], "mesh", -1)
        ahead2 = from_behind(grouped[2], "mesh", 2)
        back2 = from_behind(grouped[0], "mesh", -2)
        coef = jnp.stack([
            ahead1[0] + ahead2 + grouped[0],
            grouped[1] + ahead1[1] + back1[0],
            back1[1] + grouped[2] + back2,
        ])
        return scatter(flags, table, cell_terms, coef, coup_all, proj_values, ecell, eatom)

    psi_ext = jnp.concatenate([psi, from_behind(psi[:, :FACEP], "mesh", -1)], axis=1)
    summed = assemble(psi_ext)
    head = summed[:, :FACEP] + from_behind(summed[:, node_count:], "mesh", 1)
    tail = summed[:, node_count:] + from_behind(summed[:, :FACEP], "mesh", -1)
    summed = jnp.concatenate([head, summed[:, FACEP:node_count], tail], axis=1)
    first = ((summed + potential * psi_ext.astype(F32)) / HALFWIDTH).astype(BF16)
    summed = assemble(first)
    head = summed[:, :FACEP] + from_behind(summed[:, node_count:], "mesh", 1)
    summed = jnp.concatenate([head, summed[:, FACEP:node_count]], axis=1)
    scaled = (summed + potential[:node_count] * first[:, :node_count].astype(F32)) / HALFWIDTH
    filtered = (2.0 * scaled - psi.astype(F32)).astype(BF16)

    scale_all = 1.0 / (lax.axis_size("mesh") * node_count)
    all_states = lax.all_gather(filtered, "band", axis=0, tiled=True)
    local_sum = lax.dot_general(
        all_states, all_states, (((1,), (1,)), ((), ())), preferred_element_type=F32
    )
    correlation = lax.psum(local_sum, "mesh") * scale_all
    return (filtered, correlation)


def solution(mesh):
    return jax.shard_map(
        local,
        mesh=mesh,
        in_specs=(
            P("band", "mesh"),
            P(),
            P("mesh"),
            P(),
            P("mesh"),
            P(None, None, "mesh"),
            P("mesh"),
            P("mesh"),
            P("mesh", None, None),
        ),
        out_specs=(P("band", "mesh"), P()),
        check_vma=False,
    )
```

time: 1150 us -> 185 us (0.16)
  other arithmetic: 589 us -> 5.48 us
  local copies, waits for them, and re-layouts: 484 us -> 8.84 us
  Pallas kernels: 0 us -> 85.4 us
  waiting for transfers between devices: 1.59 us -> 13.1 us
    scatter-add x6 -> x0, other arithmetic: 584 us -> none  [the longest x2 303 us: apply_filter(): summed = summed.at[:, cell_nodes].add(cell_terms)]
    gather x9 -> x0, local copies, waits for them, and re-layouts: 408 us -> none  [the longest x4 204 us: apply_filter(): entry_vals = extended[:, entry_nodes]]
    pallas_call x0 -> x4, Pallas kernels: none -> 85.4 us  [the longest x2 48.6 us: assemble(): scatter(flags, table, cell_terms, coef, coup_all, proj_values, ecell, eatom)]
    ppermute x4 -> x15, starting transfers between devices: 10 us -> 33 us  [from_behind(): return lax.ppermute(value, axis, pairs)]
    transpose x4 -> x0, local copies, waits for them, and re-layouts: 17.2 us -> none  [apply_filter(): jnp.einsum('jke,esk->sje', proj_wide, entry_terms, precision=HIGH)]
    slice x10 -> x11, local copies, waits for them, and re-layouts: 20.9 us -> 4.51 us  [the longest x2 1.99 us: assemble(): ahead1 = from_behind(grouped[1:], 'mesh', 1)]
    mul x2 -> x0, local copies, waits for them, and re-layouts: 14.5 us -> none  [apply_filter(): jnp.einsum('ij,sjc->sic', cell_matrix, cell_vals, preferred_element_type=...]
    ppermute x8 -> x0, starting transfers between devices: 14.2 us -> none  [the longest x4 14.2 us: padded(): lax.ppermute(lax.slice_in_dim(block, 0, width, axis=dim), axis, backward)]
  transfers between devices with their start and end apart: 12 -> 15, of which waited for: 1 -> 5; matrix products, arithmetic and copies ran while one was open for 48% -> 4% of each run, Pallas kernels for 0% -> 13%
where the time goes in v1:
time: 185 us; the launch traced here: 184 us
  Pallas kernels  85.4 us (46%)
  blocking collectives  37.3 us (20%)
  starting transfers between devices  33 us (18%)
  waiting for transfers between devices  13.1 us (7%)
  local copies, waits for them, and re-layouts  8.84 us (5%)
  other arithmetic  5.48 us (3%)
    pallas_call x2, Pallas kernels, assemble(): scatter(flags, table, cell_terms, coef, coup_all, proj_values, ecell, eatom)  48.6 us
    pallas_call x2, Pallas kernels, assemble(): gather(flags, table, extended, cell_matrix, scale_row, proj_values, ecell...  36.8 us
    ppermute x15, starting transfers between devices, from_behind(): return lax.ppermute(value, axis, pairs)  33 us
    psum x1, blocking collectives, local(): correlation = lax.psum(local_sum, 'mesh') * scale_all  30 us
    ppermute x15, waiting for transfers between devices, from_behind(): return lax.ppermute(value, axis, pairs)  13.1 us
    all_gather x1, blocking collectives, local(): all_states = lax.all_gather(filtered, 'band', axis=0, tiled=True)  7.3 us
  transfers between devices with their start and end apart: 15, of which 5 were waited for; matrix products, arithmetic and copies ran while one was open for 4% of the time, Pallas kernels for 13%

profile of v1, /device:TPU:0, one launch (start us, length us, event | category | flops | bytes accessed | tf_op | source)
XLA Modules:
  0.0 184.4 jit_solution(4347446848715138114)
XLA Ops:
  1.4 5.5 %collective-permute-start = (bf16[8,1792]{1,0:T(8,128)(2,1)S(1)}, bf16[8,1792]{1,0:T(8,128)(2,1)S(1)}, u32[]{:S(2)}, u32[]{:S(2)}) collective-permute-start(bf16[8,1792]{1,0:T(8,128)(2,1)S(1)} %slice.90), channel_id=1, source_target_pairs={{0,30},{2,0},{4,2},{6,4},{8,6},{10,8},{12,10},{14,12},{16,14},{18,... | collective-permute-start | bytes 86024 | tf_op jit(solution)/shard_map/ppermute | solution.py:23
  6.9 1.0 constant_dynamic-update-slice_fusion.1
  13.1 18.4 %gather_cells.2 = (f32[1728,128]{1,0:T(8,128)}, f32[3,64,64]{2,1,0:T(8,128)}) custom-call(s32[198]{0:T(256)} %reshape.56.flags_ref, s32[18,12,128]{2,1,0:T(8,128)} %reshape.51.cn_ref, bf16[8,19712]{1,0:T(8,128)(2,1)} %copy-done.1, bf16[216,216]{1,0:T(8,128)(2,1)} %kmat_ref.3, f32[1,128]{1,0:T(1,128)} %bitcast.92, bf16[216,8,128]{2,1,0:T(8,128)(2,1)} %proj_ref.7, ...), custom_call_target="tpu_custom_call" | custom-call | tf_op jit(solution)/shard_map/gather_cells/pallas_call | solution.py:267
  31.5 1.0 fusion.20
  32.6 4.4 %collective-permute-start.3 = (f32[2,64,64]{2,1,0:T(8,128)S(1)}, f32[2,64,64]{2,1,0:T(8,128)S(1)}, u32[]{:S(2)}, u32[]{:S(2)}) collective-permute-start(f32[2,64,64]{2,1,0:T(8,128)S(1)} %get-tuple-element.38), channel_id=1, source_target_pairs={{0,30},{2,0},{4,2},{6,4},{8,6},{10,8},{12,10},{14,12},{16,14},{18,... | collective-permute-start | bytes 98312 | tf_op jit(solution)/shard_map/ppermute | solution.py:23
  37.0 4.4 %collective-permute-start.6 = (f32[64,64]{1,0:T(8,128)S(1)}, f32[64,64]{1,0:T(8,128)S(1)}, u32[]{:S(2)}, u32[]{:S(2)}) collective-permute-start(f32[64,64]{1,0:T(8,128)S(1)} %bitcast.80), channel_id=1, source_target_pairs={{0,30},{2,0},{4,2},{6,4},{8,6},{10,8},{12,10},{14,12},{16,14},{18,... | collective-permute-start | bytes 49160 | tf_op jit(solution)/shard_map/ppermute | solution.py:23
  41.6 4.7 %collective-permute-start.4 = (f32[64,64]{1,0:T(8,128)S(1)}, f32[64,64]{1,0:T(8,128)S(1)}, u32[]{:S(2)}, u32[]{:S(2)}) collective-permute-start(f32[64,64]{1,0:T(8,128)S(1)} %get-tuple-element.36), channel_id=1, source_target_pairs={{0,28},{2,30},{4,0},{6,2},{8,4},{10,6},{12,8},{14,10},{16,12},{18,... | collective-permute-start | bytes 49160 | tf_op jit(solution)/shard_map/ppermute | solution.py:23
  46.9 1.2 collective-permute-done.2
  48.9 24.3 %scatter_nodes.2 = f32[8,19712]{1,0:T(8,128)} custom-call(s32[198]{0:T(256)} %reshape.56.flags_ref, s32[18,12,128]{2,1,0:T(8,128)} %reshape.51.cn_ref, f32[1728,128]{1,0:T(8,128)} %get-tuple-element.6.ct_ref, f32[3,64,64]{2,1,0:T(8,128)} %pad_maximum_fusion.coef_ref, f32[3,64,64]{2,1,0:T(8,128)} %pad_maximum_fusion.1.coup_ref, ...), custom_call_target="tpu_custom_call" | custom-call | tf_op jit(solution)/shard_map/scatter_nodes/pallas_call | solution.py:279
  73.1 0.9 fusion.18
  74.1 4.4 %collective-permute-start.8 = (f32[8,1792]{1,0:T(8,128)S(1)}, f32[8,1792]{1,0:T(8,128)S(1)}, u32[]{:S(2)}, u32[]{:S(2)}) collective-permute-start(f32[8,1792]{1,0:T(8,128)S(1)} %get-tuple-element.24), channel_id=1, source_target_pairs={{0,30},{2,0},{4,2},{6,4},{8,6},{10,8},{12,10},{14,12},{16,14},{18,... | collective-permute-start | bytes 172040 | tf_op jit(solution)/shard_map/ppermute | solution.py:23
  78.5 1.8 collective-permute-done.7
  80.4 0.8 fusion.1.ext_ref
  81.2 18.4 %gather_cells.3 = (f32[1728,128]{1,0:T(8,128)}, f32[3,64,64]{2,1,0:T(8,128)}) custom-call(s32[198]{0:T(256)} %reshape.56.flags_ref, s32[18,12,128]{2,1,0:T(8,128)} %reshape.51.cn_ref, bf16[8,19712]{1,0:T(8,128)(2,1)} %fusion.1.ext_ref, bf16[216,216]{1,0:T(8,128)(2,1)} %kmat_ref.3, f32[1,128]{1,0:T(1,128)} %bitcast.93, bf16[216,8,128]{2,1,0:T(8,128)(2,1)} %proj_ref.7, ...), custom_call_target="tpu_custom_call" | custom-call | tf_op jit(solution)/shard_map/gather_cells/pallas_call | solution.py:267
  99.6 1.0 fusion.19
  100.7 4.5 %collective-permute-start.12 = (f32[2,64,64]{2,1,0:T(8,128)S(1)}, f32[2,64,64]{2,1,0:T(8,128)S(1)}, u32[]{:S(2)}, u32[]{:S(2)}) collective-permute-start(f32[2,64,64]{2,1,0:T(8,128)S(1)} %get-tuple-element.31), channel_id=1, source_target_pairs={{0,30},{2,0},{4,2},{6,4},{8,6},{10,8},{12,10},{14,12},{16,14},{18,... | collective-permute-start | bytes 98312 | tf_op jit(solution)/shard_map/ppermute | solution.py:23
  105.2 1.9 %collective-permute-done.10 = f32[2,64,64]{2,1,0:T(8,128)S(1)} collective-permute-done((f32[2,64,64]{2,1,0:T(8,128)S(1)}, f32[2,64,64]{2,1,0:T(8,128)S(1)}, u32[]{:S(2)}, u32[]{:S(2)}) %collective-permute-start.10) | collective-permute-done | bytes 32800 | tf_op jit(solution)/shard_map/ppermute | solution.py:23
  107.2 4.7 %collective-permute-start.13 = (f32[64,64]{1,0:T(8,128)S(1)}, f32[64,64]{1,0:T(8,128)S(1)}, u32[]{:S(2)}, u32[]{:S(2)}) collective-permute-start(f32[64,64]{1,0:T(8,128)S(1)} %get-tuple-element.29), channel_id=1, source_target_pairs={{0,28},{2,30},{4,0},{6,2},{8,4},{10,6},{12,8},{14,10},{16,12},{18,... | collective-permute-start | bytes 49160 | tf_op jit(solution)/shard_map/ppermute | solution.py:23
  111.9 1.9 %collective-permute-done.11 = f32[64,64]{1,0:T(8,128)S(1)} collective-permute-done((f32[64,64]{1,0:T(8,128)S(1)}, f32[64,64]{1,0:T(8,128)S(1)}, u32[]{:S(2)}, u32[]{:S(2)}) %collective-permute-start.11) | collective-permute-done | bytes 16416 | tf_op jit(solution)/shard_map/ppermute | solution.py:23
  114.5 24.3 %scatter_nodes.3 = f32[8,19712]{1,0:T(8,128)} custom-call(s32[198]{0:T(256)} %reshape.56.flags_ref, s32[18,12,128]{2,1,0:T(8,128)} %reshape.51.cn_ref, f32[1728,128]{1,0:T(8,128)} %get-tuple-element.8.ct_ref, f32[3,64,64]{2,1,0:T(8,128)} %pad_maximum_fusion.2.coef_ref, f32[3,64,64]{2,1,0:T(8,128)} %pad_maximum_fusion.1.coup_ref, ...), custom_call_target="tpu_custom_call" | custom-call | tf_op jit(solution)/shard_map/scatter_nodes/pallas_call | solution.py:279
  138.8 0.9 slice.130
  139.7 6.3 %collective-permute-done.14 = f32[8,1792]{1,0:T(8,128)S(1)} collective-permute-done((f32[8,1792]{1,0:T(8,128)S(1)}, f32[8,1792]{1,0:T(8,128)S(1)}, u32[]{:S(2)}, u32[]{:S(2)}) %collective-permute-start.14) | collective-permute-done | bytes 57376 | tf_op jit(solution)/shard_map/ppermute | solution.py:23
  146.2 7.3 %all_gather.3 = bf16[16,17920]{1,0:T(8,128)(2,1)S(1)} all-gather(bf16[8,17920]{1,0:T(8,128)(2,1)S(1)} %fusion.4), channel_id=1, replica_groups=mesh['mesh'=16,'band'=2] {'band'}, dimensions={0}, use_global_device_ids=true | all-gather | bytes 860160 | tf_op jit(solution)/shard_map/all_gather | solution.py:294
  153.8 30.0 %psum.7 = f32[16,16]{1,0:T(8,128)S(1)} all-reduce(f32[16,16]{1,0:T(8,128)S(1)} %fusion.21), channel_id=1, replica_groups=mesh['mesh'=16,'band'=2] {'mesh'}, use_global_device_ids=true, to_apply=%region_22.23 | all-reduce | flops 256 | bytes 2048 | tf_op jit(solution)/shard_map/psum | solution.py:298
  (91 shorter events, 9.5 us)
Async XLA Ops:
  1.4 6.5 %copy-start.9 = (s32[216,128]{1,0:T(8,128)S(1)}, s32[216,128]{1,0:T(8,128)}, u32[]{:S(2)}) copy-start(s32[216,128]{1,0:T(8,128)} %param.10) | copy-start | bytes 331780
  1.4 11.0 %collective-permute-start = (bf16[8,1792]{1,0:T(8,128)(2,1)S(1)}, bf16[8,1792]{1,0:T(8,128)(2,1)S(1)}, u32[]{:S(2)}, u32[]{:S(2)}) collective-permute-start(bf16[8,1792]{1,0:T(8,128)(2,1)S(1)} %slice.90), channel_id=1, source_target_pairs={{0,30},{2,0},{4,2},{6,4},{8,6},{10,8},{12,10},{14,12},{16,14},{18,... | collective-permute-start | bytes 86024 | tf_op jit(solution)/shard_map/ppermute | solution.py:23
  31.5 9.9 %copy-start.10 = (bf16[17920]{0:T(1024)(128)(2,1)S(1)}, bf16[17920]{0:T(1024)(128)(2,1)}, u32[]{:S(2)}) copy-start(bf16[17920]{0:T(1024)(128)(2,1)} %param.13) | copy-start | bytes 107524
  31.5 10.0 %copy-start.7 = (f32[3,64,64]{2,1,0:T(8,128)S(1)}, f32[3,64,64]{2,1,0:T(8,128)}, u32[]{:S(2)}) copy-start(f32[3,64,64]{2,1,0:T(8,128)} %get-tuple-element.7) | copy-start | bytes 147460
  32.5 9.0 %collective-permute-start.1 = (f32[2,64,64]{2,1,0:T(8,128)S(1)}, f32[2,64,64]{2,1,0:T(8,128)S(1)}, u32[]{:S(2)}, u32[]{:S(2)}) collective-permute-start(f32[2,64,64]{2,1,0:T(8,128)S(1)} %get-tuple-element.37), channel_id=1, source_target_pairs={{0,2},{2,4},{4,6},{6,8},{8,10},{10,12},{12,14},{14,16},{16,18},{18... | collective-permute-start | bytes 98312 | tf_op jit(solution)/shard_map/ppermute | solution.py:23
  32.6 8.9 %collective-permute-start.3 = (f32[2,64,64]{2,1,0:T(8,128)S(1)}, f32[2,64,64]{2,1,0:T(8,128)S(1)}, u32[]{:S(2)}, u32[]{:S(2)}) collective-permute-start(f32[2,64,64]{2,1,0:T(8,128)S(1)} %get-tuple-element.38), channel_id=1, source_target_pairs={{0,30},{2,0},{4,2},{6,4},{8,6},{10,8},{12,10},{14,12},{16,14},{18,... | collective-permute-start | bytes 98312 | tf_op jit(solution)/shard_map/ppermute | solution.py:23
  37.0 9.3 %collective-permute-start.5 = (f32[64,64]{1,0:T(8,128)S(1)}, f32[64,64]{1,0:T(8,128)S(1)}, u32[]{:S(2)}, u32[]{:S(2)}) collective-permute-start(f32[64,64]{1,0:T(8,128)S(1)} %bitcast.79), channel_id=1, source_target_pairs={{0,2},{2,4},{4,6},{6,8},{8,10},{10,12},{12,14},{14,16},{16,18},{18... | collective-permute-start | bytes 49160 | tf_op jit(solution)/shard_map/ppermute | solution.py:23
  37.0 9.3 %collective-permute-start.6 = (f32[64,64]{1,0:T(8,128)S(1)}, f32[64,64]{1,0:T(8,128)S(1)}, u32[]{:S(2)}, u32[]{:S(2)}) collective-permute-start(f32[64,64]{1,0:T(8,128)S(1)} %bitcast.80), channel_id=1, source_target_pairs={{0,30},{2,0},{4,2},{6,4},{8,6},{10,8},{12,10},{14,12},{16,14},{18,... | collective-permute-start | bytes 49160 | tf_op jit(solution)/shard_map/ppermute | solution.py:23
  41.4 37.1 %collective-permute-start.9 = (bf16[1792]{0:T(1024)(128)(2,1)S(1)}, bf16[1792]{0:T(1024)(128)(2,1)S(1)}, u32[]{:S(2)}, u32[]{:S(2)}) collective-permute-start(bf16[1792]{0:T(1024)(128)(2,1)S(1)} %slice.103), channel_id=1, source_target_pairs={{0,30},{2,0},{4,2},{6,4},{8,6},{10,8},{12,10},{14,12},{16,14},{18,... | collective-permute-start | bytes 10760 | tf_op jit(solution)/shard_map/ppermute | solution.py:23
  41.5 6.7 %collective-permute-start.2 = (f32[64,64]{1,0:T(8,128)S(1)}, f32[64,64]{1,0:T(8,128)S(1)}, u32[]{:S(2)}, u32[]{:S(2)}) collective-permute-start(f32[64,64]{1,0:T(8,128)S(1)} %get-tuple-element.34), channel_id=1, source_target_pairs={{0,4},{2,6},{4,8},{6,10},{8,12},{10,14},{12,16},{14,18},{16,20},{1... | collective-permute-start | bytes 49160 | tf_op jit(solution)/shard_map/ppermute | solution.py:23
  41.6 6.6 %collective-permute-start.4 = (f32[64,64]{1,0:T(8,128)S(1)}, f32[64,64]{1,0:T(8,128)S(1)}, u32[]{:S(2)}, u32[]{:S(2)}) collective-permute-start(f32[64,64]{1,0:T(8,128)S(1)} %get-tuple-element.36), channel_id=1, source_target_pairs={{0,28},{2,30},{4,0},{6,2},{8,4},{10,6},{12,8},{14,10},{16,12},{18,... | collective-permute-start | bytes 49160 | tf_op jit(solution)/shard_map/ppermute | solution.py:23
  74.0 6.4 %copy-start = (f32[8,19712]{1,0:T(8,128)S(1)}, f32[8,19712]{1,0:T(8,128)}, u32[]{:S(2)}) copy-start(f32[8,19712]{1,0:T(8,128)} %scatter_nodes.2) | copy-start | bytes 1892356
  74.0 6.4 %collective-permute-start.7 = (f32[8,1792]{1,0:T(8,128)S(1)}, f32[8,1792]{1,0:T(8,128)S(1)}, u32[]{:S(2)}, u32[]{:S(2)}) collective-permute-start(f32[8,1792]{1,0:T(8,128)S(1)} %get-tuple-element.23), channel_id=1, source_target_pairs={{0,2},{2,4},{4,6},{6,8},{8,10},{10,12},{12,14},{14,16},{16,18},{18... | collective-permute-start | bytes 172040 | tf_op jit(solution)/shard_map/ppermute | solution.py:23
  74.1 6.3 %collective-permute-start.8 = (f32[8,1792]{1,0:T(8,128)S(1)}, f32[8,1792]{1,0:T(8,128)S(1)}, u32[]{:S(2)}, u32[]{:S(2)}) collective-permute-start(f32[8,1792]{1,0:T(8,128)S(1)} %get-tuple-element.24), channel_id=1, source_target_pairs={{0,30},{2,0},{4,2},{6,4},{8,6},{10,8},{12,10},{14,12},{16,14},{18,... | collective-permute-start | bytes 172040 | tf_op jit(solution)/shard_map/ppermute | solution.py:23
  99.6 7.5 %copy-start.8 = (f32[3,64,64]{2,1,0:T(8,128)S(1)}, f32[3,64,64]{2,1,0:T(8,128)}, u32[]{:S(2)}) copy-start(f32[3,64,64]{2,1,0:T(8,128)} %get-tuple-element.9) | copy-start | bytes 147460
  100.6 6.4 %collective-permute-start.10 = (f32[2,64,64]{2,1,0:T(8,128)S(1)}, f32[2,64,64]{2,1,0:T(8,128)S(1)}, u32[]{:S(2)}, u32[]{:S(2)}) collective-permute-start(f32[2,64,64]{2,1,0:T(8,128)S(1)} %get-tuple-element.30), channel_id=1, source_target_pairs={{0,2},{2,4},{4,6},{6,8},{8,10},{10,12},{12,14},{14,16},{16,18},{18... | collective-permute-start | bytes 98312 | tf_op jit(solution)/shard_map/ppermute | solution.py:23
  100.7 6.4 %collective-permute-start.12 = (f32[2,64,64]{2,1,0:T(8,128)S(1)}, f32[2,64,64]{2,1,0:T(8,128)S(1)}, u32[]{:S(2)}, u32[]{:S(2)}) collective-permute-start(f32[2,64,64]{2,1,0:T(8,128)S(1)} %get-tuple-element.31), channel_id=1, source_target_pairs={{0,30},{2,0},{4,2},{6,4},{8,6},{10,8},{12,10},{14,12},{16,14},{18,... | collective-permute-start | bytes 98312 | tf_op jit(solution)/shard_map/ppermute | solution.py:23
  107.1 6.7 %collective-permute-start.11 = (f32[64,64]{1,0:T(8,128)S(1)}, f32[64,64]{1,0:T(8,128)S(1)}, u32[]{:S(2)}, u32[]{:S(2)}) collective-permute-start(f32[64,64]{1,0:T(8,128)S(1)} %get-tuple-element.27), channel_id=1, source_target_pairs={{0,4},{2,6},{4,8},{6,10},{8,12},{10,14},{12,16},{14,18},{16,20},{1... | collective-permute-start | bytes 49160 | tf_op jit(solution)/shard_map/ppermute | solution.py:23
  107.2 6.6 %collective-permute-start.13 = (f32[64,64]{1,0:T(8,128)S(1)}, f32[64,64]{1,0:T(8,128)S(1)}, u32[]{:S(2)}, u32[]{:S(2)}) collective-permute-start(f32[64,64]{1,0:T(8,128)S(1)} %get-tuple-element.29), channel_id=1, source_target_pairs={{0,28},{2,30},{4,0},{6,2},{8,4},{10,6},{12,8},{14,10},{16,12},{18,... | collective-permute-start | bytes 49160 | tf_op jit(solution)/shard_map/ppermute | solution.py:23
  114.5 31.5 %copy-start.5 = (bf16[8,17920]{1,0:T(8,128)(2,1)S(1)}, bf16[8,17920]{1,0:T(8,128)(2,1)}, u32[]{:S(2)}) copy-start(bf16[8,17920]{1,0:T(8,128)(2,1)} %param.9) | copy-start | bytes 860164
  138.8 7.2 %copy-start.4 = (f32[8,19712]{1,0:T(8,128)S(1)}, f32[8,19712]{1,0:T(8,128)}, u32[]{:S(2)}) copy-start(f32[8,19712]{1,0:T(8,128)} %scatter_nodes.3) | copy-start | bytes 1892356
  139.7 6.3 %collective-permute-start.14 = (f32[8,1792]{1,0:T(8,128)S(1)}, f32[8,1792]{1,0:T(8,128)S(1)}, u32[]{:S(2)}, u32[]{:S(2)}) collective-permute-start(f32[8,1792]{1,0:T(8,128)S(1)} %slice.130), channel_id=1, source_target_pairs={{0,2},{2,4},{4,6},{6,8},{8,10},{10,12},{12,14},{14,16},{16,18},{18... | collective-permute-start | bytes 172040 | tf_op jit(solution)/shard_map/ppermute | solution.py:23
  139.7 6.3 %copy-start.3 = (bf16[8,19712]{1,0:T(8,128)(2,1)S(1)}, bf16[8,19712]{1,0:T(8,128)(2,1)}, u32[]{:S(2)}) copy-start(bf16[8,19712]{1,0:T(8,128)(2,1)} %fusion.1.ext_ref) | copy-start | bytes 946180
  146.2 7.3 %copy-start.6 = (bf16[8,17920]{1,0:T(8,128)(2,1)}, bf16[8,17920]{1,0:T(8,128)(2,1)S(1)}, u32[]{:S(2)}) copy-start(bf16[8,17920]{1,0:T(8,128)(2,1)S(1)} %fusion.4) | copy-start | bytes 860164
  (5 other events, 16.3 us)

commit v2 on v1

--- a/solution.py
+++ b/solution.py
@@ -1,5 +1,3 @@
-import functools
-
 import jax
 import jax.numpy as jnp
 from jax import lax
@@ -15,12 +13,6 @@
 GROUP = 12
 F32 = jnp.float32
 BF16 = jnp.bfloat16
-
-
-def from_behind(value, axis, steps):
-    count = lax.axis_size(axis)
-    pairs = [(source, (source + steps) % count) for source in range(count)]
-    return lax.ppermute(value, axis, pairs)
 
 
 def fill_onehot(cn_ref, group, oh_ref):
@@ -195,6 +187,146 @@
             )
 
 
+MESH_ID = pl.DeviceIdType.MESH
+
+
+def ring_peer(steps):
+    count = lax.axis_size("mesh")
+    return lax.rem(lax.axis_index("mesh") + steps + count, count)
+
+
+def send(src, dst, sems, at, peer):
+    copy = pltpu.make_async_remote_copy(
+        src_ref=src, dst_ref=dst, send_sem=sems.at[0, at], recv_sem=sems.at[1, at],
+        device_id=peer, device_id_type=MESH_ID,
+    )
+    copy.start()
+    return copy
+
+
+def greet(peers):
+    barrier = pltpu.get_barrier_semaphore()
+    for peer in peers:
+        pl.semaphore_signal(barrier, inc=1, device_id=peer, device_id_type=MESH_ID)
+    return barrier
+
+
+def start_kernel(psi_ref, pot_ref, coup_ref, ext_ref, potx_ref, coups_ref, sems):
+    count = psi_ref.shape[1]
+    face = ext_ref.shape[1] - count
+    ahead, behind = {"mesh": ring_peer(1)}, {"mesh": ring_peer(-1)}
+    pl.semaphore_wait(greet((ahead, behind)), 2)
+    copies = [
+        send(psi_ref.at[:, :face], ext_ref.at[:, count:], sems, 0, behind),
+        send(coup_ref, coups_ref.at[0], sems, 1, ahead),
+        send(coup_ref, coups_ref.at[2], sems, 2, behind),
+        send(pot_ref.at[:, :face], potx_ref.at[:, count:], sems, 3, behind),
+    ]
+    ext_ref[:, :count] = psi_ref[...]
+    potx_ref[:, :count] = pot_ref[...]
+    coups_ref[1] = coup_ref[...]
+    for copy in copies:
+        copy.wait()
+
+
+def atoms_kernel(grouped_ref, coef_ref, left_ref, right_ref, far_ref, sems):
+    peers = [{"mesh": ring_peer(steps)} for steps in (1, -1, 2, -2)]
+    pl.semaphore_wait(greet(peers), 4)
+    copies = [
+        send(grouped_ref.at[1:3], left_ref, sems, 0, peers[0]),
+        send(grouped_ref.at[0:2], right_ref, sems, 1, peers[1]),
+        send(grouped_ref.at[2], far_ref.at[0], sems, 2, peers[2]),
+        send(grouped_ref.at[0], far_ref.at[1], sems, 3, peers[3]),
+    ]
+    for copy in copies:
+        copy.wait()
+    coef_ref[0] = left_ref[0] + far_ref[0] + grouped_ref[0]
+    coef_ref[1] = grouped_ref[1] + left_ref[1] + right_ref[0]
+    coef_ref[2] = right_ref[1] + grouped_ref[2] + far_ref[1]
+
+
+def first_kernel(y_ref, ext_ref, pot_ref, first_ref, low_ref, high_ref, sems):
+    full = y_ref.shape[1]
+    face = low_ref.shape[1]
+    count = full - face
+    ahead, behind = {"mesh": ring_peer(1)}, {"mesh": ring_peer(-1)}
+    barrier = greet((ahead, behind))
+
+    def finish(total, at):
+        scaled = (total + pot_ref[:, at] * ext_ref[:, at].astype(F32)) / HALFWIDTH
+        first_ref[:, at] = scaled.astype(BF16)
+
+    pl.semaphore_wait(barrier, 2)
+    copies = [
+        send(y_ref.at[:, count:], low_ref, sems, 0, ahead),
+        send(y_ref.at[:, :face], high_ref, sems, 1, behind),
+    ]
+    for base in range(face, count, face):
+        at = slice(base, base + face)
+        finish(y_ref[:, at], at)
+    for copy in copies:
+        copy.wait()
+    finish(y_ref[:, :face] + low_ref[...], slice(0, face))
+    finish(y_ref[:, count:] + high_ref[...], slice(count, full))
+
+
+def last_kernel(y_ref, first_ref, psi_ref, pot_ref, out_ref, corr_ref, low_ref, other_ref,
+                slots_ref, sems):
+    count = psi_ref.shape[1]
+    face = low_ref.shape[1]
+    devices = lax.axis_size("mesh")
+    bands = lax.axis_size("band")
+    me = lax.axis_index("mesh")
+    band = lax.axis_index("band")
+    partner = {"band": lax.rem(band + 1, bands)}
+    barrier = greet((partner,))
+
+    def greet_body(steps, carry):
+        pl.semaphore_signal(
+            barrier, inc=1, device_id={"mesh": lax.rem(me + steps, devices)}, device_id_type=MESH_ID
+        )
+        return carry
+
+    lax.fori_loop(1, devices, greet_body, 0)
+
+    def finish(total, at):
+        scaled = (total + pot_ref[:, at] * first_ref[:, at].astype(F32)) / HALFWIDTH
+        out_ref[:, at] = (2.0 * scaled - psi_ref[:, at].astype(F32)).astype(BF16)
+
+    pl.semaphore_wait(barrier, devices)
+    tail = send(y_ref.at[:, count:count + face], low_ref, sems, 0, {"mesh": ring_peer(1)})
+    for base in range(face, count, face):
+        at = slice(base, base + face)
+        finish(y_ref[:, at], at)
+    tail.wait()
+    finish(y_ref[:, :face] + low_ref[...], slice(0, face))
+    swap = send(out_ref, other_ref, sems, 1, partner)
+    swap.wait()
+    states = out_ref.shape[0]
+    total = jnp.zeros((bands * states, bands * states), F32)
+    for base in range(0, count, face):
+        at = slice(base, base + face)
+        own, other = out_ref[:, at].astype(F32), other_ref[:, at].astype(F32)
+        block = jnp.concatenate(
+            [jnp.where(band == 0, own, other), jnp.where(band == 0, other, own)], axis=0
+        ).astype(BF16)
+        total = total + lax.dot_general(
+            block, block, (((1,), (1,)), ((), ())), preferred_element_type=F32
+        )
+    slots_ref[me] = total
+
+    def push(steps, carry):
+        send(slots_ref.at[me], slots_ref.at[me], sems, 2, {"mesh": lax.rem(me + steps, devices)})
+        return carry
+
+    lax.fori_loop(1, devices, push, 0)
+    pltpu.make_async_remote_copy(
+        src_ref=slots_ref.at[pl.ds(0, devices - 1)], dst_ref=slots_ref.at[pl.ds(0, devices - 1)],
+        send_sem=sems.at[0, 2], recv_sem=sems.at[1, 2], device_id=partner, device_id_type=MESH_ID,
+    ).wait()
+    corr_ref[...] = jnp.sum(slots_ref[...], axis=0) * (1.0 / (devices * count))
+
+
 def local(
     psi,
     cell_nodes,
@@ -225,9 +357,7 @@
     ecell = entry_cell.reshape(1, entries)
     eatom = entry_atom.reshape(1, entries)
     coup = coupling.transpose(1, 2, 0).reshape(nproj * nproj, atoms)
-    coup_all = jnp.stack([from_behind(coup, "mesh", 1), coup, from_behind(coup, "mesh", -1)])
-    pot_ghost = from_behind(node_potential[:FACEP], "mesh", -1)
-    potential = jnp.concatenate([node_potential, pot_ghost]).astype(F32) - CENTER
+    potential = node_potential.astype(F32).reshape(1, node_count) - CENTER
 
     vmem = pl.BlockSpec(memory_space=pltpu.VMEM)
     smem = pl.BlockSpec(memory_space=pltpu.SMEM)
@@ -263,39 +393,48 @@
         name="scatter_nodes",
     )
 
-    def assemble(extended):
+    def remote(kernel, outs, n_in, scratch, copies, ident):
+        return pl.pallas_call(
+            kernel,
+            out_shape=tuple(jax.ShapeDtypeStruct(*out) for out in outs),
+            in_specs=[vmem] * n_in,
+            out_specs=(vmem,) * len(outs),
+            scratch_shapes=[pltpu.VMEM(*one) for one in scratch]
+            + [pltpu.SemaphoreType.DMA((2, copies))],
+            compiler_params=pltpu.CompilerParams(collective_id=ident, has_side_effects=True),
+            name=kernel.__name__,
+        )
+
+    pair = (nproj * states, atoms)
+
+    def assemble(extended, ident):
         cell_terms, grouped = gather(
             flags, table, extended, cell_matrix, scale_row, proj_values, ecell, eatom
         )
-        ahead1 = from_behind(grouped[1:], "mesh", 1)
-        back1 = from_behind(grouped[:2], "mesh", -1)
-        ahead2 = from_behind(grouped[2], "mesh", 2)
-        back2 = from_behind(grouped[0], "mesh", -2)
-        coef = jnp.stack([
-            ahead1[0] + ahead2 + grouped[0],
-            grouped[1] + ahead1[1] + back1[0],
-            back1[1] + grouped[2] + back2,
-        ])
+        (coef,) = remote(
+            atoms_kernel, [((3,) + pair, F32)], 1,
+            [((2,) + pair, F32), ((2,) + pair, F32), ((2,) + pair, F32)], 4, ident,
+        )(grouped)
         return scatter(flags, table, cell_terms, coef, coup_all, proj_values, ecell, eatom)
 
-    psi_ext = jnp.concatenate([psi, from_behind(psi[:, :FACEP], "mesh", -1)], axis=1)
-    summed = assemble(psi_ext)
-    head = summed[:, :FACEP] + from_behind(summed[:, node_count:], "mesh", 1)
-    tail = summed[:, node_count:] + from_behind(summed[:, :FACEP], "mesh", -1)
-    summed = jnp.concatenate([head, summed[:, FACEP:node_count], tail], axis=1)
-    first = ((summed + potential * psi_ext.astype(F32)) / HALFWIDTH).astype(BF16)
-    summed = assemble(first)
-    head = summed[:, :FACEP] + from_behind(summed[:, node_count:], "mesh", 1)
-    summed = jnp.concatenate([head, summed[:, FACEP:node_count]], axis=1)
-    scaled = (summed + potential[:node_count] * first[:, :node_count].astype(F32)) / HALFWIDTH
-    filtered = (2.0 * scaled - psi.astype(F32)).astype(BF16)
-
-    scale_all = 1.0 / (lax.axis_size("mesh") * node_count)
-    all_states = lax.all_gather(filtered, "band", axis=0, tiled=True)
-    local_sum = lax.dot_general(
-        all_states, all_states, (((1,), (1,)), ((), ())), preferred_element_type=F32
-    )
-    correlation = lax.psum(local_sum, "mesh") * scale_all
+    psi_ext, pot_ext, coup_all = remote(
+        start_kernel,
+        [((states, full), BF16), ((1, full), F32), ((3, nproj * nproj, atoms), F32)],
+        3, [], 4, 0,
+    )(psi, potential, coup)
+    face = (states, FACEP)
+    (first,) = remote(first_kernel, [((states, full), BF16)], 3, [(face, F32), (face, F32)], 2, 2)(
+        assemble(psi_ext, 1), psi_ext, pot_ext
+    )
+    bands, devices = lax.axis_size("band"), lax.axis_size("mesh")
+    square = (bands * states, bands * states)
+    filtered, correlation = remote(
+        last_kernel,
+        [((states, node_count), BF16), (square, F32)],
+        4,
+        [(face, F32), ((states, node_count), BF16), ((devices,) + square, F32)],
+        3, 4,
+    )(assemble(first, 3), first, psi, potential)
     return (filtered, correlation)
 
 

time: 185 us -> 149 us (0.81)
  Pallas kernels: 85.4 us -> 139 us
  blocking collectives: 37.3 us -> 0 us
  starting transfers between devices: 33 us -> 0 us
  waiting for transfers between devices: 13.1 us -> 0 us
  local copies, waits for them, and re-layouts: 8.84 us -> 5.76 us
  other arithmetic: 5.48 us -> 2.73 us
    pallas_call x0 -> x5, Pallas kernels: none -> 54.1 us  [the longest x1 18.9 us: local(): remote(last_kernel, [((states, node_count), BF16), (square, F32)], 4, [(f...]
    ppermute x15 -> x0, starting transfers between devices: 33 us -> none  [from_behind(): return lax.ppermute(value, axis, pairs)]
    psum x1 -> x0, blocking collectives: 30 us -> none  [local(): correlation = lax.psum(local_sum, 'mesh') * scale_all]
    ppermute x15 -> x0, waiting for transfers between devices: 13.1 us -> none  [from_behind(): return lax.ppermute(value, axis, pairs)]
    all_gather x1 -> x0, blocking collectives: 7.3 us -> none  [local(): all_states = lax.all_gather(filtered, 'band', axis=0, tiled=True)]
    slice x11 -> x0, local copies, waits for them, and re-layouts: 4.51 us -> none  [the longest x2 1.99 us: assemble(): ahead1 = from_behind(grouped[1:], 'mesh', 1)]
    another operation x5 -> x0, other arithmetic: 1.99 us -> none  [the longest x4 1.34 us: assemble(): jnp.stack([ahead1[0] + ahead2 + grouped[0], grouped[1] + ahead1[1] + back...]
  transfers between devices with their start and end apart: 15 -> 0, of which waited for: 5 -> 0; matrix products, arithmetic and copies ran while one was open for 4% -> 0% of each run, Pallas kernels for 13% -> 0%
where the time goes in v2:
time: 149 us
  Pallas kernels  139 us (93%)
  local copies, waits for them, and re-layouts  5.76 us (4%)
  other arithmetic  2.73 us (2%)
    pallas_call x2, Pallas kernels, assemble(): scatter(flags, table, cell_terms, coef, coup_all, proj_values, ecell, eatom)  48.6 us
    pallas_call x2, Pallas kernels, assemble(): gather(flags, table, extended, cell_matrix, scale_row, proj_values, ecell...  36.8 us
    pallas_call x1, Pallas kernels, local(): remote(last_kernel, [((states, node_count), BF16), (square, F32)], 4, [(f...  18.9 us
    pallas_call x2, Pallas kernels, assemble(): remote(atoms_kernel, [((3,) + pair, F32)], 1, [((2,) + pair, F32), ((2,)...  17.1 us
    pallas_call x1, Pallas kernels, local(): remote(start_kernel, [((states, full), BF16), ((1, full), F32), ((3, npro...  9.61 us
    pallas_call x1, Pallas kernels, local(): remote(first_kernel, [((states, full), BF16)], 3, [(face, F32), (face, F3...  8.43 us

profile of v2, /device:TPU:0, one launch (start us, length us, event | category | flops | bytes accessed | tf_op | source)
XLA Modules:
  0.0 148.8 jit_solution(18418771204104579967)
XLA Ops:
  0.6 1.4 compare_reduce_fusion
  2.2 0.1 reduce_or.208
  2.4 0.1 reduce_or.205
  2.6 0.1 reduce_or.202
  2.8 0.1 reduce_or.199
  3.1 0.1 reduce_or.160
  3.3 0.1 reduce_or.157
  4.2 0.1 reduce_or.136
  4.4 0.1 reduce_or.130
  4.7 0.7 reshape.41.flags_ref
  5.4 0.7 sub.14.pot_ref
  6.1 0.2 copy-done
  6.3 0.7 reshape.36.cn_ref
  6.9 9.6 %start_kernel.1 = (bf16[8,19712]{1,0:T(8,128)(2,1)}, f32[1,19712]{1,0:T(1,128)}, f32[3,64,64]{2,1,0:T(8,128)}) custom-call(bf16[8,17920]{1,0:T(8,128)(2,1)} %psi_ref.3, f32[1,17920]{1,0:T(1,128)} %sub.14.pot_ref, f32[64,64]{1,0:T(8,128)} %bitcast.17), custom_call_target="tpu_custom_call" | custom-call | tf_op jit(solution)/shard_map/start_kernel/pallas_call | solution.py:420
  16.6 18.4 %gather_cells.2 = (f32[1728,128]{1,0:T(8,128)}, f32[3,64,64]{2,1,0:T(8,128)}) custom-call(s32[198]{0:T(256)} %reshape.41.flags_ref, s32[18,12,128]{2,1,0:T(8,128)} %reshape.36.cn_ref, bf16[8,19712]{1,0:T(8,128)(2,1)} %get-tuple-element.9.ext_ref, bf16[216,216]{1,0:T(8,128)(2,1)} %kmat_ref.3, f32[1,128]{1,0:T(1,128)} %bitcast.26, ...), custom_call_target="tpu_custom_call" | custom-call | tf_op jit(solution)/shard_map/gather_cells/pallas_call | solution.py:411
  35.0 8.6 %atoms_kernel.2.coef_ref = f32[3,64,64]{2,1,0:T(8,128)} custom-call(f32[3,64,64]{2,1,0:T(8,128)} %get-tuple-element.11.grouped_ref), custom_call_target="tpu_custom_call" | custom-call | tf_op jit(solution)/shard_map/atoms_kernel/pallas_call | solution.py:414
  43.5 24.3 %scatter_nodes.2.y_ref = f32[8,19712]{1,0:T(8,128)} custom-call(s32[198]{0:T(256)} %reshape.41.flags_ref, s32[18,12,128]{2,1,0:T(8,128)} %reshape.36.cn_ref, f32[1728,128]{1,0:T(8,128)} %get-tuple-element.10.ct_ref, f32[3,64,64]{2,1,0:T(8,128)} %atoms_kernel.2.coef_ref, f32[3,64,64]{2,1,0:T(8,128)} %get-tuple-element.12.coup_ref, ...), custom_call_target="tpu_custom_call" | custom-call | tf_op jit(solution)/shard_map/scatter_nodes/pallas_call | solution.py:418
  67.8 8.4 %first_kernel.1.ext_ref.first_ref = bf16[8,19712]{1,0:T(8,128)(2,1)} custom-call(f32[8,19712]{1,0:T(8,128)} %scatter_nodes.2.y_ref, bf16[8,19712]{1,0:T(8,128)(2,1)} %get-tuple-element.9.ext_ref, f32[1,19712]{1,0:T(1,128)} %get-tuple-element.13.pot_ref), custom_call_target="tpu_custom_call" | custom-call | tf_op jit(solution)/shard_map/first_kernel/pallas_call | solution.py:426
  76.3 18.4 %gather_cells.3 = (f32[1728,128]{1,0:T(8,128)}, f32[3,64,64]{2,1,0:T(8,128)}) custom-call(s32[198]{0:T(256)} %reshape.41.flags_ref, s32[18,12,128]{2,1,0:T(8,128)} %reshape.36.cn_ref, bf16[8,19712]{1,0:T(8,128)(2,1)} %first_kernel.1.ext_ref.first_ref, bf16[216,216]{1,0:T(8,128)(2,1)} %kmat_ref.3, f32[1,128]{1,0:T(1,128)} %bitcast.27, ...), custom_call_target="tpu_custom_call" | custom-call | tf_op jit(solution)/shard_map/gather_cells/pallas_call | solution.py:411
  94.7 8.6 %atoms_kernel.3.coef_ref = f32[3,64,64]{2,1,0:T(8,128)} custom-call(f32[3,64,64]{2,1,0:T(8,128)} %get-tuple-element.15.grouped_ref), custom_call_target="tpu_custom_call" | custom-call | tf_op jit(solution)/shard_map/atoms_kernel/pallas_call | solution.py:414
  103.3 24.3 %scatter_nodes.3.y_ref = f32[8,19712]{1,0:T(8,128)} custom-call(s32[198]{0:T(256)} %reshape.41.flags_ref, s32[18,12,128]{2,1,0:T(8,128)} %reshape.36.cn_ref, f32[1728,128]{1,0:T(8,128)} %get-tuple-element.14.ct_ref, f32[3,64,64]{2,1,0:T(8,128)} %atoms_kernel.3.coef_ref, f32[3,64,64]{2,1,0:T(8,128)} %get-tuple-element.12.coup_ref, ...), custom_call_target="tpu_custom_call" | custom-call | tf_op jit(solution)/shard_map/scatter_nodes/pallas_call | solution.py:418
  127.6 18.9 %last_kernel.1 = (bf16[8,17920]{1,0:T(8,128)(2,1)}, f32[16,16]{1,0:T(8,128)}) custom-call(f32[8,19712]{1,0:T(8,128)} %scatter_nodes.3.y_ref, bf16[8,19712]{1,0:T(8,128)(2,1)} %first_kernel.1.ext_ref.first_ref, bf16[8,17920]{1,0:T(8,128)(2,1)} %psi_ref.3, f32[1,17920]{1,0:T(1,128)} %sub.14.pot_ref), custom_call_target="tpu_custom_call" | custom-call | tf_op jit(solution)/shard_map/last_kernel/pallas_call | solution.py:431
  146.5 1.7 %copy.14 = bf16[8,17920]{1,0:T(8,128)(2,1)} copy(bf16[8,17920]{1,0:T(8,128)(2,1)} %get-tuple-element.29) | data formatting | bytes 573440
  148.2 0.6 copy.15
  (23 shorter events, 1.6 us)
Async XLA Ops:
  4.1 1.3 copy-start.1
  5.4 0.9 copy-start
  146.5 1.7 %copy-start.2 = (f32[16,16]{1,0:T(8,128)S(1)}, f32[16,16]{1,0:T(8,128)}, u32[]{:S(2)}) copy-start(f32[16,16]{1,0:T(8,128)} %get-tuple-element.30) | copy-start | bytes 3076

commit v3 on v2

--- a/solution.py
+++ b/solution.py
@@ -27,85 +27,54 @@
     return lax.shift_right_logical(rows, 8)
 
 
-def gather_kernel(flags_ref, cn_ref, ext_ref, kmat_ref, scale_ref, proj_ref, ecell_ref,
-                  eatom_ref, ct_ref, grouped_ref, lhs_ref, oh_ref, xs_ref, es_ref):
+def gather_kernel(sched_ref, cn_ref, ext_ref, xs_ref, lhs_ref, oh_ref):
     states = ext_ref.shape[0]
-    chunks, rows_in_chunk, _ = lhs_ref.shape
-    layers = rows_in_chunk // states
+    chunks = lhs_ref.shape[0] - 1
+    layers = ext_ref.shape[1] // (chunks * WIDE)
     groups = cn_ref.shape[0]
     cells = cn_ref.shape[2]
-    width = groups * GROUP
+    padded = lhs_ref.shape[1]
+    slots = sched_ref.shape[0] // groups
+    lhs_ref[...] = jnp.zeros_like(lhs_ref)
     for c in range(chunks):
         base = c * layers * WIDE
         parts = [
             ext_ref[:, base + l * WIDE:base + (l + 1) * WIDE].astype(F32) for l in range(layers)
         ]
+        parts.append(jnp.zeros((padded - layers * states, WIDE), F32))
         lhs_ref[c] = jnp.concatenate(parts, axis=0).astype(BF16)
+    xs_ref[...] = jnp.zeros_like(xs_ref)
 
     def group_body(g, carry):
         lo = fill_onehot(cn_ref, g, oh_ref)
 
-        def chunk_body(c, inner):
-            @pl.when(flags_ref[g * chunks + c] > 0)
-            def _():
-                out = jnp.dot(lhs_ref[c], oh_ref[...], preferred_element_type=F32)
-                for jj in range(GROUP):
-                    where = pl.ds(pl.multiple_of((g * GROUP + jj) * states, states), states)
-                    value = xs_ref[where, :]
-                    row = lo[jj:jj + 1, :] - c * layers
+        def pair_body(r, inner):
+            first = sched_ref[g * slots + 2 * r]
+            second = sched_ref[g * slots + 2 * r + 1]
+            lhs = jnp.concatenate([lhs_ref[first], lhs_ref[second]], axis=0)
+            out = jnp.dot(lhs, oh_ref[...], preferred_element_type=F32)
+            for jj in range(GROUP):
+                where = pl.ds(pl.multiple_of((g * GROUP + jj) * states, states), states)
+                value = xs_ref[where, :]
+                lanes = slice(jj * cells, (jj + 1) * cells)
+                for half, chunk in enumerate((first, second)):
+                    row = lo[jj:jj + 1, :] - chunk * layers
                     for l in range(layers):
-                        value = jnp.where(
-                            row == l,
-                            out[l * states:(l + 1) * states, jj * cells:(jj + 1) * cells],
-                            value,
-                        )
-                    xs_ref[where, :] = value
+                        at = half * padded + l * states
+                        value = jnp.where(row == l, out[at:at + states, lanes], value)
+                xs_ref[where, :] = value
             return inner
 
-        return lax.fori_loop(0, chunks, chunk_body, carry)
-
-    xs_ref[...] = jnp.zeros_like(xs_ref)
+        pairs = lax.shift_right_logical(sched_ref[g * slots + slots - 1] + 1, 1)
+        return lax.fori_loop(0, pairs, pair_body, carry)
+
     lax.fori_loop(0, groups, group_body, 0)
 
-    cell_ids = lax.broadcasted_iota(jnp.int32, (cells, ecell_ref.shape[1]), 0)
-    spread = jnp.where(cell_ids == ecell_ref[...], 1.0, 0.0).astype(BF16)
-    es_ref[...] = jnp.dot(xs_ref[...].astype(BF16), spread, preferred_element_type=F32)
-
-    kmat = kmat_ref[...]
-    scale = scale_ref[...]
-    for s in range(0, states, 2):
-        pair = jnp.concatenate(
-            [xs_ref[pl.ds(s, width, stride=states), :], xs_ref[pl.ds(s + 1, width, stride=states), :]],
-            axis=1,
-        ).astype(BF16)
-        out = jnp.dot(kmat, pair, preferred_element_type=F32)
-        ct_ref[pl.ds(s, width, stride=states), :] = out[:, :cells] * scale
-        ct_ref[pl.ds(s + 1, width, stride=states), :] = out[:, cells:] * scale
-
-    nproj = proj_ref.shape[1]
-    entries = ecell_ref.shape[1]
-
-    def partial_body(j, accs):
-        values = es_ref[pl.ds(pl.multiple_of(j * states, states), states), :]
-        proj = proj_ref[j].astype(F32)
-        return tuple(acc + proj[k:k + 1, :] * values for k, acc in enumerate(accs))
-
-    zero = jnp.zeros((states, entries), F32)
-    accs = lax.fori_loop(0, width, partial_body, (zero,) * nproj, unroll=4)
-    partial_sum = jnp.concatenate(accs, axis=0)
-    atoms = grouped_ref.shape[2]
-    slot_ids = lax.broadcasted_iota(jnp.int32, (atoms, entries), 0)
-    for g in range(3):
-        chosen = jnp.where(eatom_ref[...] == slot_ids + g * atoms, 1.0, 0.0)
-        grouped_ref[g] = lax.dot_general(
-            partial_sum, chosen, (((1,), (1,)), ((), ())), precision=HIGH,
-            preferred_element_type=F32,
-        )
-
-
-def scatter_kernel(flags_ref, cn_ref, ct_ref, coef_ref, coup_ref, proj_ref, ecell_ref,
+
+def scatter_kernel(sched_ref, cn_ref, ct_ref, coef_ref, coup_ref, proj_ref, ecell_ref,
                    eatom_ref, y_ref, oh_ref, ns_ref, v_ref, lhs_ref, acc_ref):
     chunks, rows_in_chunk, _ = acc_ref.shape
+    chunks = chunks - 1
     groups = cn_ref.shape[0]
     cells = cn_ref.shape[2]
     width = groups * GROUP
@@ -153,29 +122,34 @@
         + lax.dot_general(node_rest, spread, back, preferred_element_type=F32)
     )
     acc_ref[...] = jnp.zeros_like(acc_ref)
+    slots = sched_ref.shape[0] // groups
 
     def group_body(g, carry):
         lo = fill_onehot(cn_ref, g, oh_ref)
 
-        def chunk_body(c, inner):
-            @pl.when(flags_ref[g * chunks + c] > 0)
-            def _():
-                for jj in range(GROUP):
-                    start = pl.multiple_of((g * GROUP + jj) * states, states)
-                    value = v_ref[pl.ds(start, states), :]
-                    top = value.astype(BF16).astype(F32)
-                    both = jnp.concatenate([top, value - top], axis=0)
-                    row = lo[jj:jj + 1, :] - c * layers
+        def pair_body(r, inner):
+            first = sched_ref[g * slots + 2 * r]
+            second = sched_ref[g * slots + 2 * r + 1]
+            for jj in range(GROUP):
+                start = pl.multiple_of((g * GROUP + jj) * states, states)
+                value = v_ref[pl.ds(start, states), :]
+                top = value.astype(BF16).astype(F32)
+                both = jnp.concatenate([top, value - top], axis=0)
+                lanes = slice(jj * cells, (jj + 1) * cells)
+                for half, chunk in enumerate((first, second)):
+                    row = lo[jj:jj + 1, :] - chunk * layers
                     for l in range(layers):
-                        lhs_ref[l * 2 * states:(l + 1) * 2 * states, jj * cells:(jj + 1) * cells] = (
+                        at = half * rows_in_chunk + l * 2 * states
+                        lhs_ref[at:at + 2 * states, lanes] = (
                             jnp.where(row == l, both, 0.0).astype(BF16)
                         )
-                acc_ref[c] += lax.dot_general(
-                    lhs_ref[...], oh_ref[...], back, preferred_element_type=F32
-                )
+            out = lax.dot_general(lhs_ref[...], oh_ref[...], back, preferred_element_type=F32)
+            acc_ref[first] += out[:rows_in_chunk]
+            acc_ref[second] += out[rows_in_chunk:]
             return inner
 
-        return lax.fori_loop(0, chunks, chunk_body, carry)
+        pairs = lax.shift_right_logical(sched_ref[g * slots + slots - 1] + 1, 1)
+        return lax.fori_loop(0, pairs, pair_body, carry)
 
     lax.fori_loop(0, groups, group_body, 0)
     for c in range(chunks):
@@ -229,15 +203,50 @@
         copy.wait()
 
 
-def atoms_kernel(grouped_ref, coef_ref, left_ref, right_ref, far_ref, sems):
+def atoms_kernel(xs_ref, kmat_ref, scale_ref, proj_ref, ecell_ref, eatom_ref, ct_ref, coef_ref,
+                 es_ref, grouped_ref, left_ref, right_ref, far_ref, sems):
     peers = [{"mesh": ring_peer(steps)} for steps in (1, -1, 2, -2)]
-    pl.semaphore_wait(greet(peers), 4)
+    barrier = greet(peers)
+    width, nproj, entries = proj_ref.shape
+    cells = xs_ref.shape[1]
+    states = xs_ref.shape[0] // width
+    cell_ids = lax.broadcasted_iota(jnp.int32, (cells, entries), 0)
+    spread = jnp.where(cell_ids == ecell_ref[...], 1.0, 0.0).astype(BF16)
+    es_ref[...] = jnp.dot(xs_ref[...].astype(BF16), spread, preferred_element_type=F32)
+
+    def partial_body(j, accs):
+        values = es_ref[pl.ds(pl.multiple_of(j * states, states), states), :]
+        proj = proj_ref[j].astype(F32)
+        return tuple(acc + proj[k:k + 1, :] * values for k, acc in enumerate(accs))
+
+    zero = jnp.zeros((states, entries), F32)
+    accs = lax.fori_loop(0, width, partial_body, (zero,) * nproj, unroll=4)
+    partial_sum = jnp.concatenate(accs, axis=0)
+    atoms = grouped_ref.shape[2]
+    slot_ids = lax.broadcasted_iota(jnp.int32, (atoms, entries), 0)
+    for g in range(3):
+        chosen = jnp.where(eatom_ref[...] == slot_ids + g * atoms, 1.0, 0.0)
+        grouped_ref[g] = lax.dot_general(
+            partial_sum, chosen, (((1,), (1,)), ((), ())), precision=HIGH,
+            preferred_element_type=F32,
+        )
+    pl.semaphore_wait(barrier, 4)
     copies = [
         send(grouped_ref.at[1:3], left_ref, sems, 0, peers[0]),
         send(grouped_ref.at[0:2], right_ref, sems, 1, peers[1]),
         send(grouped_ref.at[2], far_ref.at[0], sems, 2, peers[2]),
         send(grouped_ref.at[0], far_ref.at[1], sems, 3, peers[3]),
     ]
+    kmat = kmat_ref[...]
+    scale = scale_ref[...]
+    for s in range(0, states, 2):
+        pair = jnp.concatenate(
+            [xs_ref[pl.ds(s, width, stride=states), :], xs_ref[pl.ds(s + 1, width, stride=states), :]],
+            axis=1,
+        ).astype(BF16)
+        out = jnp.dot(kmat, pair, preferred_element_type=F32)
+        ct_ref[pl.ds(s, width, stride=states), :] = out[:, :cells] * scale
+        ct_ref[pl.ds(s + 1, width, stride=states), :] = out[:, cells:] * scale
     for copy in copies:
         copy.wait()
     coef_ref[0] = left_ref[0] + far_ref[0] + grouped_ref[0]
@@ -256,12 +265,16 @@
         scaled = (total + pot_ref[:, at] * ext_ref[:, at].astype(F32)) / HALFWIDTH
         first_ref[:, at] = scaled.astype(BF16)
 
+    middle = face * (1 + (count // face - 1) // 2)
+    for base in range(face, middle, face):
+        at = slice(base, base + face)
+        finish(y_ref[:, at], at)
     pl.semaphore_wait(barrier, 2)
     copies = [
         send(y_ref.at[:, count:], low_ref, sems, 0, ahead),
         send(y_ref.at[:, :face], high_ref, sems, 1, behind),
     ]
-    for base in range(face, count, face):
+    for base in range(middle, count, face):
         at = slice(base, base + face)
         finish(y_ref[:, at], at)
     for copy in copies:
@@ -293,26 +306,33 @@
         scaled = (total + pot_ref[:, at] * first_ref[:, at].astype(F32)) / HALFWIDTH
         out_ref[:, at] = (2.0 * scaled - psi_ref[:, at].astype(F32)).astype(BF16)
 
-    pl.semaphore_wait(barrier, devices)
-    tail = send(y_ref.at[:, count:count + face], low_ref, sems, 0, {"mesh": ring_peer(1)})
     for base in range(face, count, face):
         at = slice(base, base + face)
         finish(y_ref[:, at], at)
-    tail.wait()
-    finish(y_ref[:, :face] + low_ref[...], slice(0, face))
-    swap = send(out_ref, other_ref, sems, 1, partner)
-    swap.wait()
+    pl.semaphore_wait(barrier, devices)
+    tail = send(y_ref.at[:, count:count + face], low_ref, sems, 0, {"mesh": ring_peer(1)})
+    swap = send(out_ref.at[:, face:], other_ref.at[:, face:], sems, 1, partner)
     states = out_ref.shape[0]
-    total = jnp.zeros((bands * states, bands * states), F32)
-    for base in range(0, count, face):
+
+    def gram(base):
         at = slice(base, base + face)
         own, other = out_ref[:, at].astype(F32), other_ref[:, at].astype(F32)
         block = jnp.concatenate(
             [jnp.where(band == 0, own, other), jnp.where(band == 0, other, own)], axis=0
         ).astype(BF16)
-        total = total + lax.dot_general(
+        return lax.dot_general(
             block, block, (((1,), (1,)), ((), ())), preferred_element_type=F32
         )
+
+    tail.wait()
+    finish(y_ref[:, :face] + low_ref[...], slice(0, face))
+    edge = send(out_ref.at[:, :face], other_ref.at[:, :face], sems, 3, partner)
+    swap.wait()
+    total = gram(face)
+    for base in range(2 * face, count, face):
+        total = total + gram(base)
+    edge.wait()
+    total = total + gram(0)
     slots_ref[me] = total
 
     def push(steps, carry):
@@ -352,7 +372,17 @@
     owner = table // FACEP
     flags = jnp.stack(
         [jnp.any(owner == c, axis=(1, 2)) for c in range(chunks)], axis=1
-    ).astype(jnp.int32).reshape(groups * chunks)
+    ).astype(jnp.int32)
+    ids = jnp.arange(chunks, dtype=jnp.int32)
+    rank = jnp.sum(flags[:, None, :] * (ids[None, :] < ids[:, None]), axis=2)
+    places = jnp.arange(chunks + 1, dtype=jnp.int32)
+    used = flags[:, :, None] * (rank[:, :, None] == places)
+    listed = chunks + jnp.sum(used * (ids[None, :, None] - chunks), axis=1)
+    listed = jnp.concatenate(
+        [listed, jnp.full((groups, 1), chunks, jnp.int32), jnp.sum(flags, axis=1, keepdims=True)],
+        axis=1,
+    )
+    sched = listed.astype(jnp.int32).reshape(groups * (chunks + 3))
     scale_row = cell_scale.reshape(1, cells)
     ecell = entry_cell.reshape(1, entries)
     eatom = entry_atom.reshape(1, entries)
@@ -362,19 +392,15 @@
     vmem = pl.BlockSpec(memory_space=pltpu.VMEM)
     smem = pl.BlockSpec(memory_space=pltpu.SMEM)
 
+    padded = (layers * states + 15) // 16 * 16
     gather = pl.pallas_call(
         gather_kernel,
-        out_shape=(
-            jax.ShapeDtypeStruct((width * states, cells), F32),
-            jax.ShapeDtypeStruct((3, nproj * states, atoms), F32),
-        ),
-        in_specs=[smem] + [vmem] * 7,
-        out_specs=(vmem, vmem),
+        out_shape=jax.ShapeDtypeStruct((width * states, cells), F32),
+        in_specs=[smem] + [vmem] * 2,
+        out_specs=vmem,
         scratch_shapes=[
-            pltpu.VMEM((chunks, layers * states, WIDE), BF16),
+            pltpu.VMEM((chunks + 1, padded, WIDE), BF16),
             pltpu.VMEM((WIDE, span), BF16),
-            pltpu.VMEM((width * states, cells), F32),
-            pltpu.VMEM((width * states, entries), F32),
         ],
         name="gather_cells",
     )
@@ -387,8 +413,8 @@
             pltpu.VMEM((WIDE, span), BF16),
             pltpu.VMEM((width * states, entries), F32),
             pltpu.VMEM((width * states, cells), F32),
-            pltpu.VMEM((layers * 2 * states, span), BF16),
-            pltpu.VMEM((chunks, layers * 2 * states, WIDE), F32),
+            pltpu.VMEM((2 * layers * 2 * states, span), BF16),
+            pltpu.VMEM((chunks + 1, layers * 2 * states, WIDE), F32),
         ],
         name="scatter_nodes",
     )
@@ -408,14 +434,13 @@
     pair = (nproj * states, atoms)
 
     def assemble(extended, ident):
-        cell_terms, grouped = gather(
-            flags, table, extended, cell_matrix, scale_row, proj_values, ecell, eatom
-        )
-        (coef,) = remote(
-            atoms_kernel, [((3,) + pair, F32)], 1,
-            [((2,) + pair, F32), ((2,) + pair, F32), ((2,) + pair, F32)], 4, ident,
-        )(grouped)
-        return scatter(flags, table, cell_terms, coef, coup_all, proj_values, ecell, eatom)
+        values = gather(sched, table, extended)
+        cell_terms, coef = remote(
+            atoms_kernel, [((width * states, cells), F32), ((3,) + pair, F32)], 6,
+            [((width * states, entries), F32), ((3,) + pair, F32)] + [((2,) + pair, F32)] * 3,
+            4, ident,
+        )(values, cell_matrix, scale_row, proj_values, ecell, eatom)
+        return scatter(sched, table, cell_terms, coef, coup_all, proj_values, ecell, eatom)
 
     psi_ext, pot_ext, coup_all = remote(
         start_kernel,
@@ -433,7 +458,7 @@
         [((states, node_count), BF16), (square, F32)],
         4,
         [(face, F32), ((states, node_count), BF16), ((devices,) + square, F32)],
-        3, 4,
+        4, 4,
     )(assemble(first, 3), first, psi, potential)
     return (filtered, correlation)
 

time: 149 us -> 116 us (0.78)
  Pallas kernels: 139 us -> 106 us
    pallas_call x6, Pallas kernels: 103 us -> 70.7 us  [the longest x2 31.1 us: assemble(): scatter(sched, table, cell_terms, coef, coup_all, proj_values, ecell, eatom)]
    pallas_call x1, Pallas kernels: 18.9 us -> 17.2 us  [local(): remote(last_kernel, [((states, node_count), BF16), (square, F32)], 4, [(f...]
where the time goes in v3:
time: 116 us; the launch traced here: 115 us
  Pallas kernels  106 us (91%)
  local copies, waits for them, and re-layouts  5.84 us (5%)
  other arithmetic  3.01 us (3%)
    pallas_call x2, Pallas kernels, assemble(): scatter(sched, table, cell_terms, coef, coup_all, proj_values, ecell, eatom)  31.1 us
    pallas_call x2, Pallas kernels, assemble(): values = gather(sched, table, extended)  19.9 us
    pallas_call x2, Pallas kernels, assemble(): remote(atoms_kernel, [((width * states, cells), F32), ((3,) + pair, F32)]...  19.6 us
    pallas_call x1, Pallas kernels, local(): remote(last_kernel, [((states, node_count), BF16), (square, F32)], 4, [(f...  17.2 us
    pallas_call x1, Pallas kernels, local(): remote(start_kernel, [((states, full), BF16), ((1, full), F32), ((3, npro...  9.6 us
    pallas_call x1, Pallas kernels, local(): remote(first_kernel, [((states, full), BF16)], 3, [(face, F32), (face, F3...  8.28 us
    reduce_or x12, other arithmetic, local(): jnp.any(owner == c, axis=(1, 2))  2.71 us
    unnamed x8, local copies, waits for them, and re-layouts  2.52 us

profile of v3, /device:TPU:0, one launch (start us, length us, event | category | flops | bytes accessed | tf_op | source)
XLA Modules:
  0.0 115.5 jit_solution(18138304772654815148)
XLA Ops:
  0.7 1.4 %compare_reduce_fusion = (pred[216]{0:T(512)(128)(4,1)S(1)}, pred[216]{0:T(512)(128)(4,1)S(1)}, pred[216]{0:T(512)(128)(4,1)S(1)}, pred[216]{0:T(512)(128)(4,1)S...) fusion(s32[216,128]{1,0:T(8,128)} %param.10), kind=kLoop, calls=%fused_computation.4 | loop fusion | flops 827064 | bytes 112968 | tf_op jit(solution)/shard_map/reduce_or | solution.py:374
  2.2 0.1 reduce_or.208
  2.5 0.1 reduce_or.205
  2.7 0.1 reduce_or.202
  2.9 0.1 reduce_or.199
  3.1 0.1 reduce_or.160
  3.4 0.1 reduce_or.157
  3.8 0.1 reduce_or.145
  4.0 0.1 reduce_or.142
  5.1 0.7 reshape.232.sched_ref
  5.8 0.7 sub.18.pot_ref
  6.5 0.2 copy-done
  6.7 0.7 reshape.233.cn_ref
  7.3 9.6 %start_kernel.1 = (bf16[8,19712]{1,0:T(8,128)(2,1)}, f32[1,19712]{1,0:T(1,128)}, f32[3,64,64]{2,1,0:T(8,128)}) custom-call(bf16[8,17920]{1,0:T(8,128)(2,1)} %psi_ref.3, f32[1,17920]{1,0:T(1,128)} %sub.18.pot_ref, f32[64,64]{1,0:T(8,128)} %bitcast.19), custom_call_target="tpu_custom_call" | custom-call | tf_op jit(solution)/shard_map/start_kernel/pallas_call | solution.py:445
  17.0 10.0 %gather_cells.2.xs_ref = f32[1728,128]{1,0:T(8,128)} custom-call(s32[252]{0:T(256)} %reshape.232.sched_ref, s32[18,12,128]{2,1,0:T(8,128)} %reshape.233.cn_ref, bf16[8,19712]{1,0:T(8,128)(2,1)} %get-tuple-element.9.ext_ref), custom_call_target="tpu_custom_call" | custom-call | tf_op jit(solution)/shard_map/gather_cells/pallas_call | solution.py:437
  26.9 10.3 %atoms_kernel.2 = (f32[1728,128]{1,0:T(8,128)}, f32[3,64,64]{2,1,0:T(8,128)}) custom-call(f32[1728,128]{1,0:T(8,128)} %gather_cells.2.xs_ref, bf16[216,216]{1,0:T(8,128)(2,1)} %kmat_ref.3, f32[1,128]{1,0:T(1,128)} %bitcast.28, bf16[216,8,128]{2,1,0:T(8,128)(2,1)} %proj_ref.7, s32[1,128]{1,0:T(1,128)} %bitcast.20, s32[1,128]{1,0:T(1,128)} %bitcast.24), custom_call_target="tpu_custom_call" | custom-call | tf_op jit(solution)/shard_map/atoms_kernel/pallas_call | solution.py:438
  37.2 15.5 %scatter_nodes.2.y_ref = f32[8,19712]{1,0:T(8,128)} custom-call(s32[252]{0:T(256)} %reshape.232.sched_ref, s32[18,12,128]{2,1,0:T(8,128)} %reshape.233.cn_ref, f32[1728,128]{1,0:T(8,128)} %get-tuple-element.10.ct_ref, f32[3,64,64]{2,1,0:T(8,128)} %get-tuple-element.11.coef_ref, f32[3,64,64]{2,1,0:T(8,128)} %get-tuple-element.12.coup_ref, ...), custom_call_target="tpu_custom_call" | custom-call | tf_op jit(solution)/shard_map/scatter_nodes/pallas_call | solution.py:443
  52.7 8.3 %first_kernel.1.ext_ref.first_ref = bf16[8,19712]{1,0:T(8,128)(2,1)} custom-call(f32[8,19712]{1,0:T(8,128)} %scatter_nodes.2.y_ref, bf16[8,19712]{1,0:T(8,128)(2,1)} %get-tuple-element.9.ext_ref, f32[1,19712]{1,0:T(1,128)} %get-tuple-element.13.pot_ref), custom_call_target="tpu_custom_call" | custom-call | tf_op jit(solution)/shard_map/first_kernel/pallas_call | solution.py:451
  61.0 10.0 %gather_cells.3.xs_ref = f32[1728,128]{1,0:T(8,128)} custom-call(s32[252]{0:T(256)} %reshape.232.sched_ref, s32[18,12,128]{2,1,0:T(8,128)} %reshape.233.cn_ref, bf16[8,19712]{1,0:T(8,128)(2,1)} %first_kernel.1.ext_ref.first_ref), custom_call_target="tpu_custom_call" | custom-call | tf_op jit(solution)/shard_map/gather_cells/pallas_call | solution.py:437
  71.0 9.4 %atoms_kernel.3 = (f32[1728,128]{1,0:T(8,128)}, f32[3,64,64]{2,1,0:T(8,128)}) custom-call(f32[1728,128]{1,0:T(8,128)} %gather_cells.3.xs_ref, bf16[216,216]{1,0:T(8,128)(2,1)} %kmat_ref.3, f32[1,128]{1,0:T(1,128)} %bitcast.29, bf16[216,8,128]{2,1,0:T(8,128)(2,1)} %proj_ref.7, s32[1,128]{1,0:T(1,128)} %bitcast.22, s32[1,128]{1,0:T(1,128)} %bitcast.26), custom_call_target="tpu_custom_call" | custom-call | tf_op jit(solution)/shard_map/atoms_kernel/pallas_call | solution.py:438
  80.4 15.5 %scatter_nodes.3.y_ref = f32[8,19712]{1,0:T(8,128)} custom-call(s32[252]{0:T(256)} %reshape.232.sched_ref, s32[18,12,128]{2,1,0:T(8,128)} %reshape.233.cn_ref, f32[1728,128]{1,0:T(8,128)} %get-tuple-element.14.ct_ref, f32[3,64,64]{2,1,0:T(8,128)} %get-tuple-element.15.coef_ref, f32[3,64,64]{2,1,0:T(8,128)} %get-tuple-element.12.coup_ref, ...), custom_call_target="tpu_custom_call" | custom-call | tf_op jit(solution)/shard_map/scatter_nodes/pallas_call | solution.py:443
  95.9 17.2 %last_kernel.1 = (bf16[8,17920]{1,0:T(8,128)(2,1)}, f32[16,16]{1,0:T(8,128)}) custom-call(f32[8,19712]{1,0:T(8,128)} %scatter_nodes.3.y_ref, bf16[8,19712]{1,0:T(8,128)(2,1)} %first_kernel.1.ext_ref.first_ref, bf16[8,17920]{1,0:T(8,128)(2,1)} %psi_ref.3, f32[1,17920]{1,0:T(1,128)} %sub.18.pot_ref), custom_call_target="tpu_custom_call" | custom-call | tf_op jit(solution)/shard_map/last_kernel/pallas_call | solution.py:456
  113.2 1.7 %copy.20 = bf16[8,17920]{1,0:T(8,128)(2,1)} copy(bf16[8,17920]{1,0:T(8,128)(2,1)} %get-tuple-element.29) | data formatting | bytes 573440
  114.9 0.6 copy.21
  (31 shorter events, 2.0 us)
Async XLA Ops:
  4.9 0.9 copy-start.1
  5.8 0.9 copy-start
  113.2 1.7 %copy-start.2 = (f32[16,16]{1,0:T(8,128)S(1)}, f32[16,16]{1,0:T(8,128)}, u32[]{:S(2)}) copy-start(f32[16,16]{1,0:T(8,128)} %get-tuple-element.30) | copy-start | bytes 3076

commit v4 on v3

--- a/solution.py
+++ b/solution.py
@@ -10,7 +10,7 @@
 HALFWIDTH = 2.5
 HIGH = lax.Precision.HIGHEST
 WIDE = 256
-GROUP = 12
+GROUP = 36
 F32 = jnp.float32
 BF16 = jnp.bfloat16
 
@@ -109,7 +109,7 @@
         ns_ref[pl.ds(pl.multiple_of(j * states, states), states), :] = total
         return carry
 
-    lax.fori_loop(0, width, node_body, 0, unroll=4)
+    lax.fori_loop(0, width, node_body, 0, unroll=8)
     cell_ids = lax.broadcasted_iota(jnp.int32, (cells, entries), 0)
     spread = jnp.where(cell_ids == ecell_ref[...], 1.0, 0.0).astype(BF16)
     back = (((1,), (1,)), ((), ()))
@@ -220,7 +220,7 @@
         return tuple(acc + proj[k:k + 1, :] * values for k, acc in enumerate(accs))
 
     zero = jnp.zeros((states, entries), F32)
-    accs = lax.fori_loop(0, width, partial_body, (zero,) * nproj, unroll=4)
+    accs = lax.fori_loop(0, width, partial_body, (zero,) * nproj, unroll=8)
     partial_sum = jnp.concatenate(accs, axis=0)
     atoms = grouped_ref.shape[2]
     slot_ids = lax.broadcasted_iota(jnp.int32, (atoms, entries), 0)
@@ -324,13 +324,13 @@
             block, block, (((1,), (1,)), ((), ())), preferred_element_type=F32
         )
 
-    tail.wait()
-    finish(y_ref[:, :face] + low_ref[...], slice(0, face))
-    edge = send(out_ref.at[:, :face], other_ref.at[:, :face], sems, 3, partner)
     swap.wait()
     total = gram(face)
     for base in range(2 * face, count, face):
         total = total + gram(base)
+    tail.wait()
+    finish(y_ref[:, :face] + low_ref[...], slice(0, face))
+    edge = send(out_ref.at[:, :face], other_ref.at[:, :face], sems, 3, partner)
     edge.wait()
     total = total + gram(0)
     slots_ref[me] = total

time: 116 us -> 109 us (0.940)
  Pallas kernels: 106 us -> 98.4 us
    pallas_call x2, Pallas kernels: 31.1 us -> 26.1 us  [assemble(): scatter(sched, table, cell_terms, coef, coup_all, proj_values, ecell, eatom)]
    pallas_call x2, Pallas kernels: 19.9 us -> 15.6 us  [assemble(): values = gather(sched, table, extended)]
    pallas_call x1, Pallas kernels: 17.2 us -> 19.3 us  [local(): remote(last_kernel, [((states, node_count), BF16), (square, F32)], 4, [(f...]
where the time goes in v4:
time: 109 us; the launch traced here: 108 us
  Pallas kernels  98.4 us (90%)
  local copies, waits for them, and re-layouts  5.71 us (5%)
  other arithmetic  3.29 us (3%)
    pallas_call x2, Pallas kernels, assemble(): scatter(sched, table, cell_terms, coef, coup_all, proj_values, ecell, eatom)  26.1 us
    pallas_call x2, Pallas kernels, assemble(): remote(atoms_kernel, [((width * states, cells), F32), ((3,) + pair, F32)]...  19.5 us
    pallas_call x1, Pallas kernels, local(): remote(last_kernel, [((states, node_count), BF16), (square, F32)], 4, [(f...  19.3 us
    pallas_call x2, Pallas kernels, assemble(): values = gather(sched, table, extended)  15.6 us
    pallas_call x1, Pallas kernels, local(): remote(start_kernel, [((states, full), BF16), ((1, full), F32), ((3, npro...  9.6 us
    pallas_call x1, Pallas kernels, local(): remote(first_kernel, [((states, full), BF16)], 3, [(face, F32), (face, F3...  8.28 us
    reduce_or x12, other arithmetic, local(): jnp.any(owner == c, axis=(1, 2))  2.77 us
    unnamed x8, local copies, waits for them, and re-layouts  2.52 us

profile of v4, /device:TPU:0, one launch (start us, length us, event | category | flops | bytes accessed | tf_op | source)
XLA Modules:
  0.0 108.1 jit_solution(11263371179133082087)
XLA Ops:
  0.7 1.4 %compare_reduce_fusion = (pred[216]{0:T(512)(128)(4,1)S(1)}, pred[216]{0:T(512)(128)(4,1)S(1)}, pred[216]{0:T(512)(128)(4,1)S(1)}, pred[216]{0:T(512)(128)(4,1)S...) fusion(s32[216,128]{1,0:T(8,128)} %param.10), kind=kLoop, calls=%fused_computation.4 | loop fusion | flops 827064 | bytes 112968 | tf_op jit(solution)/shard_map/reduce_or | solution.py:374
  2.4 0.1 reduce_or.205
  2.6 0.1 reduce_or.202
  3.1 0.1 reduce_or.160
  3.3 0.1 reduce_or.157
  3.5 0.1 reduce_or.151
  3.7 0.1 reduce_or.145
  3.9 0.1 reduce_or.142
  4.8 0.3 multiply_reduce_fusion.1
  5.2 0.6 reshape.232.sched_ref
  5.9 0.7 sub.18.pot_ref
  6.5 0.2 copy-done
  6.7 0.7 reshape.233.cn_ref
  7.4 9.6 %start_kernel.1 = (bf16[8,19712]{1,0:T(8,128)(2,1)}, f32[1,19712]{1,0:T(1,128)}, f32[3,64,64]{2,1,0:T(8,128)}) custom-call(bf16[8,17920]{1,0:T(8,128)(2,1)} %psi_ref.3, f32[1,17920]{1,0:T(1,128)} %sub.18.pot_ref, f32[64,64]{1,0:T(8,128)} %bitcast.19), custom_call_target="tpu_custom_call" | custom-call | tf_op jit(solution)/shard_map/start_kernel/pallas_call | solution.py:445
  17.0 7.8 %gather_cells.2.xs_ref = f32[1728,128]{1,0:T(8,128)} custom-call(s32[84]{0:T(128)} %reshape.232.sched_ref, s32[6,36,128]{2,1,0:T(8,128)} %reshape.233.cn_ref, bf16[8,19712]{1,0:T(8,128)(2,1)} %get-tuple-element.9.ext_ref), custom_call_target="tpu_custom_call" | custom-call | tf_op jit(solution)/shard_map/gather_cells/pallas_call | solution.py:437
  24.8 10.1 %atoms_kernel.2 = (f32[1728,128]{1,0:T(8,128)}, f32[3,64,64]{2,1,0:T(8,128)}) custom-call(f32[1728,128]{1,0:T(8,128)} %gather_cells.2.xs_ref, bf16[216,216]{1,0:T(8,128)(2,1)} %kmat_ref.3, f32[1,128]{1,0:T(1,128)} %bitcast.28, bf16[216,8,128]{2,1,0:T(8,128)(2,1)} %proj_ref.7, s32[1,128]{1,0:T(1,128)} %bitcast.20, s32[1,128]{1,0:T(1,128)} %bitcast.24), custom_call_target="tpu_custom_call" | custom-call | tf_op jit(solution)/shard_map/atoms_kernel/pallas_call | solution.py:438
  34.9 13.1 %scatter_nodes.2.y_ref = f32[8,19712]{1,0:T(8,128)} custom-call(s32[84]{0:T(128)} %reshape.232.sched_ref, s32[6,36,128]{2,1,0:T(8,128)} %reshape.233.cn_ref, f32[1728,128]{1,0:T(8,128)} %get-tuple-element.10.ct_ref, f32[3,64,64]{2,1,0:T(8,128)} %get-tuple-element.11.coef_ref, f32[3,64,64]{2,1,0:T(8,128)} %get-tuple-element.12.coup_ref, ...), custom_call_target="tpu_custom_call" | custom-call | tf_op jit(solution)/shard_map/scatter_nodes/pallas_call | solution.py:443
  48.0 8.3 %first_kernel.1.ext_ref.first_ref = bf16[8,19712]{1,0:T(8,128)(2,1)} custom-call(f32[8,19712]{1,0:T(8,128)} %scatter_nodes.2.y_ref, bf16[8,19712]{1,0:T(8,128)(2,1)} %get-tuple-element.9.ext_ref, f32[1,19712]{1,0:T(1,128)} %get-tuple-element.13.pot_ref), custom_call_target="tpu_custom_call" | custom-call | tf_op jit(solution)/shard_map/first_kernel/pallas_call | solution.py:451
  56.3 7.8 %gather_cells.3.xs_ref = f32[1728,128]{1,0:T(8,128)} custom-call(s32[84]{0:T(128)} %reshape.232.sched_ref, s32[6,36,128]{2,1,0:T(8,128)} %reshape.233.cn_ref, bf16[8,19712]{1,0:T(8,128)(2,1)} %first_kernel.1.ext_ref.first_ref), custom_call_target="tpu_custom_call" | custom-call | tf_op jit(solution)/shard_map/gather_cells/pallas_call | solution.py:437
  64.1 9.4 %atoms_kernel.3 = (f32[1728,128]{1,0:T(8,128)}, f32[3,64,64]{2,1,0:T(8,128)}) custom-call(f32[1728,128]{1,0:T(8,128)} %gather_cells.3.xs_ref, bf16[216,216]{1,0:T(8,128)(2,1)} %kmat_ref.3, f32[1,128]{1,0:T(1,128)} %bitcast.29, bf16[216,8,128]{2,1,0:T(8,128)(2,1)} %proj_ref.7, s32[1,128]{1,0:T(1,128)} %bitcast.22, s32[1,128]{1,0:T(1,128)} %bitcast.26), custom_call_target="tpu_custom_call" | custom-call | tf_op jit(solution)/shard_map/atoms_kernel/pallas_call | solution.py:438
  73.4 13.1 %scatter_nodes.3.y_ref = f32[8,19712]{1,0:T(8,128)} custom-call(s32[84]{0:T(128)} %reshape.232.sched_ref, s32[6,36,128]{2,1,0:T(8,128)} %reshape.233.cn_ref, f32[1728,128]{1,0:T(8,128)} %get-tuple-element.14.ct_ref, f32[3,64,64]{2,1,0:T(8,128)} %get-tuple-element.15.coef_ref, f32[3,64,64]{2,1,0:T(8,128)} %get-tuple-element.12.coup_ref, ...), custom_call_target="tpu_custom_call" | custom-call | tf_op jit(solution)/shard_map/scatter_nodes/pallas_call | solution.py:443
  86.5 19.3 %last_kernel.1 = (bf16[8,17920]{1,0:T(8,128)(2,1)}, f32[16,16]{1,0:T(8,128)}) custom-call(f32[8,19712]{1,0:T(8,128)} %scatter_nodes.3.y_ref, bf16[8,19712]{1,0:T(8,128)(2,1)} %first_kernel.1.ext_ref.first_ref, bf16[8,17920]{1,0:T(8,128)(2,1)} %psi_ref.3, f32[1,17920]{1,0:T(1,128)} %sub.18.pot_ref), custom_call_target="tpu_custom_call" | custom-call | tf_op jit(solution)/shard_map/last_kernel/pallas_call | solution.py:456
  105.8 1.7 %copy.18 = bf16[8,17920]{1,0:T(8,128)(2,1)} copy(bf16[8,17920]{1,0:T(8,128)(2,1)} %get-tuple-element.29) | data formatting | bytes 573440
  107.5 0.6 copy.19
  (32 shorter events, 2.0 us)
Async XLA Ops:
  4.7 1.1 %copy-start.1 = (bf16[17920]{0:T(1024)(128)(2,1)S(1)}, bf16[17920]{0:T(1024)(128)(2,1)}, u32[]{:S(2)}) copy-start(bf16[17920]{0:T(1024)(128)(2,1)} %param.13) | copy-start | bytes 107524
  5.8 0.9 copy-start
  105.8 1.7 %copy-start.2 = (f32[16,16]{1,0:T(8,128)S(1)}, f32[16,16]{1,0:T(8,128)}, u32[]{:S(2)}) copy-start(f32[16,16]{1,0:T(8,128)} %get-tuple-element.30) | copy-start | bytes 3076
